TPU v7x, 32 devices: a whole 2x2x4 slice. The times are simulated.
32 devices in a mesh: fsdp: 4 (over x, core), context: 2 (over y), tensor: 4 (over z).
Axes of the slice: x: 2, y: 2, z: 4, core: 2. Of those that a mesh axis runs over, the one named last changes fastest.
Arguments:
- tokens: bfloat16 [8192, 1024], P(('fsdp', 'context')), may hold values from -6 to 6
- cotangent: bfloat16 [8192, 1024], P(('fsdp', 'context')), may hold values from -6 to 6
- segments: int32 [8192], P(('fsdp', 'context')), may hold values from 0 to 3, as said below
- positions: int32 [8192], P(('fsdp', 'context')), may hold values from 0 to 1535, as said below
- parents: int32 [4, 4], P('fsdp'), may hold values from 0 to 3, as said below
- block_lists: int32 [16, 3], P(('fsdp', 'context')), may hold values from -1 to 3, as said below
- project_weight: bfloat16 [1024, 3, 1024], P('fsdp', None, 'tensor'), may hold values from -0.1875 to 0.1875
- project_bias: float32 [3, 1024], P(None, 'tensor'), may hold values from -3 to 3
- dense_weight: bfloat16 [1024, 1024], P('tensor', 'fsdp'), may hold values from -3 to 3
- dense_bias: float32 [1024], replicated, may hold values from -3 to 3
- up_weight: bfloat16 [1024, 4096], P('fsdp', 'tensor'), may hold values from -0.1875 to 0.1875
- up_bias: float32 [4096], P('tensor'), may hold values from -3 to 3
- down_weight: bfloat16 [4096, 1024], P('tensor', 'fsdp'), may hold values from -0.09375 to 0.09375
- down_bias: float32 [1024], replicated, may hold values from -3 to 3
- first_gain: float32 [1024], replicated, may hold values from 0.1 to 1.9
- first_shift: float32 [1024], replicated, may hold values from -3 to 3
- second_gain: float32 [1024], replicated, may hold values from 0.1 to 1.9
- second_shift: float32 [1024], replicated, may hold values from -3 to 3
Outputs:
- layer_out: bfloat16 [8192, 1024], P(('fsdp', 'context'))
- tokens_grad: bfloat16 [8192, 1024], P(('fsdp', 'context'))
- project_weight_grad: float32 [1024, 3, 1024], P('fsdp', None, 'tensor')
- project_bias_grad: float32 [3, 1024], P(None, 'tensor')
- dense_weight_grad: float32 [1024, 1024], P('tensor', 'fsdp')
- dense_bias_grad: float32 [1024], replicated
- up_weight_grad: float32 [1024, 4096], P('fsdp', 'tensor')
- up_bias_grad: float32 [4096], P('tensor')
- down_weight_grad: float32 [4096, 1024], P('tensor', 'fsdp')
- down_bias_grad: float32 [1024], replicated
- first_gain_grad: float32 [1024], replicated
- first_shift_grad: float32 [1024], replicated
- second_gain_grad: float32 [1024], replicated
- second_shift_grad: float32 [1024], replicated
Inputs may be any that keep to these rules, and one draw needn't show every extreme that they name: `segments`: every aligned block of 512 tokens lies in one segment; a tree has one trunk of 1 block, 1 branches and 2 leaves of one block each, its blocks in any order. The trunk's blocks hold positions 0 to 511, a branch's block starts at 512, a leaf's at 1024; within a block positions rise by one. `parents`: the trunk is its own parent, each branch's parent is the trunk, each leaf's parent a branch, each branch the parent of two leaves. `block_lists`: each row holds its own block and every block of the segments above it on its path, each once in some order, then -1 to the end; a listed block other than its own lies wholly in an ancestor segment with smaller positions.
All inputs are finite; a program needn't handle non-finite values.
Results may differ from a plain program's by a relative error of at most 0.012.
The roundings to bfloat16 on the way count: a program that leaves them out, or rounds other values in their place, can miss the bound.
Values may be sent and summed in bfloat16 or wider, within the bound.
No kernel may reach another device: no remote copies, remote signals or barrier semaphores. Data moves between devices by JAX's collectives and lax.ppermute only.
A program may use at most 128 MiB of HBM per device.

v0:
```python
from functools import partial

import jax
import jax.numpy as jnp
from jax import lax
from jax.sharding import PartitionSpec as P

HD = 64
ROT = 16
BLK = 512


epsilon = 1e-05
masked = -1e30


def norm_layer(values_in, gain_row, shift_row):
    row_mean = jnp.mean(values_in, axis=-1, keepdims=True)
    centered = values_in - row_mean
    variance = jnp.mean(centered * centered, axis=-1, keepdims=True)
    return centered * lax.rsqrt(variance + epsilon) * gain_row + shift_row


def angles(path_pos):
    frequency = jnp.exp(-jnp.log(10000.0) * jnp.arange(ROT // 2, dtype=jnp.float32) * 2.0 / ROT)
    angle_rows = path_pos.astype(jnp.float32)[:, None] * frequency[None, :]
    return (jnp.cos(angle_rows), jnp.sin(angle_rows))


def rotate(values_in, cos_rows, sin_rows):
    rot_half = ROT // 2
    lower_part = values_in[..., :rot_half]
    upper_part = values_in[..., rot_half:ROT]
    cos_part = cos_rows[:, None, :]
    sin_part = sin_rows[:, None, :]
    return jnp.concatenate(
        [
            lower_part * cos_part - upper_part * sin_part,
            upper_part * cos_part + lower_part * sin_part,
            values_in[..., ROT:],
        ],
        axis=-1,
    )


def unrotate(grads_in, cos_rows, sin_rows):
    rot_half = ROT // 2
    lower_part = grads_in[..., :rot_half]
    upper_part = grads_in[..., rot_half:ROT]
    cos_part = cos_rows[:, None, :]
    sin_part = sin_rows[:, None, :]
    return jnp.concatenate(
        [
            lower_part * cos_part + upper_part * sin_part,
            upper_part * cos_part - lower_part * sin_part,
            grads_in[..., ROT:],
        ],
        axis=-1,
    )


def fetch_block(whole, index, heads_here):
    start_row = jnp.maximum(index, 0) * BLK
    return lax.dynamic_slice_in_dim(whole, start_row, BLK, 0).reshape(BLK, heads_here, HD)


def visible_scores(query_block, key_block, index, own_slot, score_scale):
    scores = (
        jnp.einsum("qhd,khd->hqk", query_block, key_block, preferred_element_type=jnp.float32)
        * score_scale
    )
    row_ids = lax.broadcasted_iota(jnp.int32, scores.shape[1:], 0)
    col_ids = lax.broadcasted_iota(jnp.int32, scores.shape[1:], 1)
    keep = (index >= 0) & ((index != own_slot) | (col_ids <= row_ids))
    return (jnp.where(keep[None], scores, masked), keep[None])


def attend_forward(query_block, listing, own_slot, key_all, value_all, heads_here, score_scale):

    def first_pass(carry, index):
        row_top, total = carry
        scores, keep = visible_scores(
            query_block, fetch_block(key_all, index, heads_here), index, own_slot, score_scale
        )
        new_top = jnp.maximum(row_top, jnp.max(scores, axis=-1, keepdims=True))
        total = total * jnp.exp(row_top - new_top) + jnp.sum(
            jnp.where(keep, jnp.exp(scores - new_top), 0.0), axis=-1, keepdims=True
        )
        return ((new_top, total), None)

    start_state = (
        jnp.full((heads_here, BLK, 1), masked, jnp.float32),
        jnp.zeros((heads_here, BLK, 1), jnp.float32),
    )
    (row_top, total), unused = lax.scan(first_pass, start_state, listing)
    log_total = row_top + jnp.log(total)

    def second_pass(result, index):
        scores, keep = visible_scores(
            query_block, fetch_block(key_all, index, heads_here), index, own_slot, score_scale
        )
        probability = jnp.where(keep, jnp.exp(scores - log_total), 0.0).astype(jnp.bfloat16)
        value_block = fetch_block(value_all, index, heads_here)
        return (
            result
            + jnp.einsum(
                "hqk,khd->qhd", probability, value_block, preferred_element_type=jnp.float32
            ),
            None,
        )

    result, unused = lax.scan(second_pass, jnp.zeros((BLK, heads_here, HD), jnp.float32), listing)
    return (result, log_total)


def attend_backward(
    query_block,
    grad_block,
    listing,
    own_slot,
    log_total,
    key_all,
    value_all,
    key_grads,
    value_grads,
    heads_here,
    score_scale,
):

    def delta_pass(delta, index):
        scores, keep = visible_scores(
            query_block, fetch_block(key_all, index, heads_here), index, own_slot, score_scale
        )
        probability = jnp.where(keep, jnp.exp(scores - log_total), 0.0)
        prob_grad = jnp.einsum(
            "qhd,khd->hqk",
            grad_block,
            fetch_block(value_all, index, heads_here),
            preferred_element_type=jnp.float32,
        )
        return (delta + jnp.sum(probability * prob_grad, axis=-1, keepdims=True), None)

    delta, unused = lax.scan(delta_pass, jnp.zeros((heads_here, BLK, 1), jnp.float32), listing)

    def grad_pass(carry, index):
        query_grad, key_grads, value_grads = carry
        key_block = fetch_block(key_all, index, heads_here)
        value_block = fetch_block(value_all, index, heads_here)
        scores, keep = visible_scores(query_block, key_block, index, own_slot, score_scale)
        probability = jnp.where(keep, jnp.exp(scores - log_total), 0.0)
        prob_grad = jnp.einsum(
            "qhd,khd->hqk", grad_block, value_block, preferred_element_type=jnp.float32
        )
        score_grad = (probability * (prob_grad - delta)).astype(jnp.bfloat16)
        query_grad = (
            query_grad
            + jnp.einsum("hqk,khd->qhd", score_grad, key_block, preferred_element_type=jnp.float32)
            * score_scale
        )
        key_piece = (
            jnp.einsum("hqk,qhd->khd", score_grad, query_block, preferred_element_type=jnp.float32)
            * score_scale
        )
        value_piece = jnp.einsum(
            "hqk,qhd->khd",
            probability.astype(jnp.bfloat16),
            grad_block,
            preferred_element_type=jnp.float32,
        )
        start_row = jnp.maximum(index, 0) * BLK
        key_old = lax.dynamic_slice_in_dim(key_grads, start_row, BLK, 0)
        value_old = lax.dynamic_slice_in_dim(value_grads, start_row, BLK, 0)
        key_grads = lax.dynamic_update_slice_in_dim(
            key_grads, key_old + key_piece.reshape(BLK, -1), start_row, 0
        )
        value_grads = lax.dynamic_update_slice_in_dim(
            value_grads, value_old + value_piece.reshape(BLK, -1), start_row, 0
        )
        return ((query_grad, key_grads, value_grads), None)

    start_state = (jnp.zeros((BLK, heads_here, HD), jnp.float32), key_grads, value_grads)
    (query_grad, key_grads, value_grads), unused = lax.scan(grad_pass, start_state, listing)
    return (query_grad, key_grads, value_grads)


def body(
    tokens,
    cotangent,
    segments,
    positions,
    parents,
    block_lists,
    project_weight,
    project_bias,
    dense_weight,
    dense_bias,
    up_weight,
    up_bias,
    down_weight,
    down_bias,
    first_gain,
    first_shift,
    second_gain,
    second_shift,
):
    row_count = tokens.shape[0]
    heads_here = project_weight.shape[2] // HD
    head_width = heads_here * HD
    block_count = row_count // BLK
    score_scale = HD ** (-0.5)
    full_project, full_dense, full_up, full_down = (
        lax.all_gather(project_weight, "fsdp", axis=0, tiled=True),
        lax.all_gather(dense_weight, "fsdp", axis=1, tiled=True),
        lax.all_gather(up_weight, "fsdp", axis=0, tiled=True),
        lax.all_gather(down_weight, "fsdp", axis=1, tiled=True),
    )
    inputs = tokens.astype(jnp.float32)
    normed_one, pull_one = jax.vjp(norm_layer, inputs, first_gain, first_shift)
    normed_two, pull_two = jax.vjp(norm_layer, inputs, second_gain, second_shift)
    normed_one = normed_one.astype(jnp.bfloat16)
    normed_two = normed_two.astype(jnp.bfloat16)
    projected = (
        jnp.einsum("td,dcj->tcj", normed_one, full_project, preferred_element_type=jnp.float32)
        + project_bias[None]
    )
    cos_rows, sin_rows = angles(positions)
    queries = rotate(projected[:, 0].reshape(row_count, heads_here, HD), cos_rows, sin_rows).astype(
        jnp.bfloat16
    )
    key_rows = (
        rotate(projected[:, 1].reshape(row_count, heads_here, HD), cos_rows, sin_rows)
        .astype(jnp.bfloat16)
        .reshape(row_count, head_width)
    )
    value_rows = projected[:, 2].astype(jnp.bfloat16)
    key_all, value_all = (
        lax.all_gather(key_rows, "context", axis=0, tiled=True),
        lax.all_gather(value_rows, "context", axis=0, tiled=True),
    )
    first_slot = lax.axis_index("context") * block_count
    context_blocks = []
    log_totals = []
    for block_index in range(block_count):
        query_block = queries[block_index * BLK : (block_index + 1) * BLK]
        result, log_total = attend_forward(
            query_block,
            block_lists[block_index],
            first_slot + block_index,
            key_all,
            value_all,
            heads_here,
            score_scale,
        )
        context_blocks.append(result)
        log_totals.append(log_total)
    context_low = (
        jnp.concatenate(context_blocks, axis=0).reshape(row_count, head_width).astype(jnp.bfloat16)
    )
    hidden = jnp.dot(normed_two, full_up, preferred_element_type=jnp.float32) + up_bias
    activated, pull_gelu = jax.vjp(partial(jax.nn.gelu, approximate=False), hidden)
    activated = activated.astype(jnp.bfloat16)
    partial_out = jnp.dot(context_low, full_dense, preferred_element_type=jnp.float32) + jnp.dot(
        activated, full_down, preferred_element_type=jnp.float32
    )
    summed = lax.psum(partial_out, "tensor")
    layer_out = (inputs + summed + dense_bias + down_bias).astype(jnp.bfloat16)
    upstream = cotangent.astype(jnp.float32)
    bias_total = jnp.sum(upstream, axis=0)
    context_grad = jnp.einsum(
        "te,je->tj", cotangent, full_dense, preferred_element_type=jnp.float32
    ).astype(jnp.bfloat16)
    dense_grad = jnp.einsum("tj,te->je", context_low, cotangent, preferred_element_type=jnp.float32)
    activated_grad = jnp.einsum(
        "te,fe->tf", cotangent, full_down, preferred_element_type=jnp.float32
    )
    hidden_grad = pull_gelu(activated_grad)[0].astype(jnp.bfloat16)
    down_grad = jnp.einsum("tf,te->fe", activated, cotangent, preferred_element_type=jnp.float32)
    up_grad = jnp.einsum("td,tf->df", normed_two, hidden_grad, preferred_element_type=jnp.float32)
    up_bias_grad = jnp.sum(hidden_grad.astype(jnp.float32), axis=0)
    second_part = jnp.einsum("tf,df->td", hidden_grad, full_up, preferred_element_type=jnp.float32)
    key_grads = jnp.zeros(key_all.shape, jnp.float32)
    value_grads = jnp.zeros(value_all.shape, jnp.float32)
    context_grad_heads = context_grad.reshape(row_count, heads_here, HD)
    query_grads = []
    for block_index in range(block_count):
        query_block = queries[block_index * BLK : (block_index + 1) * BLK]
        grad_block = context_grad_heads[block_index * BLK : (block_index + 1) * BLK]
        query_grad, key_grads, value_grads = attend_backward(
            query_block,
            grad_block,
            block_lists[block_index],
            first_slot + block_index,
            log_totals[block_index],
            key_all,
            value_all,
            key_grads,
            value_grads,
            heads_here,
            score_scale,
        )
        query_grads.append(query_grad)
    key_local, value_local = (
        lax.psum_scatter(key_grads, "context", scatter_dimension=0, tiled=True),
        lax.psum_scatter(value_grads, "context", scatter_dimension=0, tiled=True),
    )
    query_local = jnp.concatenate(query_grads, axis=0)
    projected_grad = jnp.stack(
        [
            unrotate(query_local, cos_rows, sin_rows).reshape(row_count, head_width),
            unrotate(key_local.reshape(row_count, heads_here, HD), cos_rows, sin_rows).reshape(
                row_count, head_width
            ),
            value_local,
        ],
        axis=1,
    ).astype(jnp.bfloat16)
    project_grad = jnp.einsum(
        "td,tcj->dcj", normed_one, projected_grad, preferred_element_type=jnp.float32
    )
    project_bias_grad = jnp.sum(projected_grad.astype(jnp.float32), axis=0)
    first_part = jnp.einsum(
        "tcj,dcj->td", projected_grad, full_project, preferred_element_type=jnp.float32
    )
    first_grad, second_grad = lax.psum((first_part, second_part), "tensor")
    input_one, gain_one, shift_one = pull_one(first_grad)
    input_two, gain_two, shift_two = pull_two(second_grad)
    tokens_grad = (upstream + input_one + input_two).astype(jnp.bfloat16)
    small = lax.psum(
        (project_bias_grad, bias_total, up_bias_grad, gain_one, shift_one, gain_two, shift_two),
        ("fsdp", "context"),
    )
    bias_sums = (small[0], small[1], small[2])
    norm_sums = (small[3], small[4], small[5], small[6])
    shards = (
        lax.psum_scatter(project_grad, "fsdp", scatter_dimension=0, tiled=True),
        lax.psum_scatter(dense_grad, "fsdp", scatter_dimension=1, tiled=True),
        lax.psum_scatter(up_grad, "fsdp", scatter_dimension=0, tiled=True),
        lax.psum_scatter(down_grad, "fsdp", scatter_dimension=1, tiled=True),
    )
    shards = lax.psum((shards[0], shards[1], shards[2], shards[3]), "context")
    return (
        layer_out,
        tokens_grad,
        shards[0],
        bias_sums[0],
        shards[1],
        bias_sums[1],
        shards[2],
        bias_sums[2],
        shards[3],
        bias_sums[1],
        norm_sums[0],
        norm_sums[1],
        norm_sums[2],
        norm_sums[3],
    )


def solution(mesh):
    in_specs = (
        P(("fsdp", "context"), None),
        P(("fsdp", "context"), None),
        P(("fsdp", "context")),
        P(("fsdp", "context")),
        P("fsdp", None),
        P(("fsdp", "context"), None),
        P("fsdp", None, "tensor"),
        P(None, "tensor"),
        P("tensor", "fsdp"),
        P(),
        P("fsdp", "tensor"),
        P("tensor"),
        P("tensor", "fsdp"),
        P(),
        P(),
        P(),
        P(),
        P(),
    )
    out_specs = (
        P(("fsdp", "context"), None),
        P(("fsdp", "context"), None),
        P("fsdp", None, "tensor"),
        P(None, "tensor"),
        P("tensor", "fsdp"),
        P(),
        P("fsdp", "tensor"),
        P("tensor"),
        P("tensor", "fsdp"),
        P(),
        P(),
        P(),
        P(),
        P(),
    )
    return jax.shard_map(body, mesh=mesh, in_specs=in_specs, out_specs=out_specs, check_vma=False)
```

profile of v0, /device:TPU:0, one launch (start us, length us, event | category | flops | bytes accessed | tf_op | source)
XLA Modules:
  0.0 967.3 jit_solution(9456298475303301639)
XLA Ops:
  13.6 19.2 %all-gather.7.cloned.1.call-done = bf16[1024,3,256]{0,2,1:T(8,128)(2,1)} async-done(((bf16[256,3,256]{0,2,1:T(8,128)(2,1)}), bf16[1024,3,256]{0,2,1:T(8,128)(2,1)}) %all-gather.7.cloned.1.call-update) | async-done | bytes 1572880 | tf_op jit(solution)/shard_map/all_gather | solution.py:212
  41.9 7.2 all_gather.21
  51.6 8.1 all-gather.9.cloned.1.call-done
  59.7 17.4 %while.100 = (s32[]{:T(128)}, f32[4,512,1]{1,0,2:T(4,128)S(1)}, f32[4,512,1]{1,0,2:T(4,128)S(1)}, s32[3]{0:T(128)S(1)}, s32[]{:T(128)}, /*index=5*/bf16[2048,256...) while((s32[]{:T(128)}, f32[4,512,1]{1,0,2:T(4,128)S(1)}, ...), condition=%wide.region_5.6_spmd.clone, body=%wide.region_2.5_spmd.clone.sunk | while | flops 143403008 | bytes 10330334 | solution.py:95
  77.2 6.0 all-gather.15.cloned.1.call-done
  83.2 21.2 %while.104 = (s32[]{:T(128)}, f32[4,512,1]{1,2,0:T(1,128)S(1)}, s32[3]{0:T(128)S(1)}, s32[]{:T(128)}, bf16[2048,256]{0,1:T(8,128)(2,1)}, /*index=5*/bf16[512,4,6...) while((s32[]{:T(128)}, f32[4,512,1]{1,2,0:T(1,128)S(1)}, ...), condition=%wide.region_17.18_spmd.clone, body=%wide.region_15.17_spmd.clone.sunk | while | flops 275515392 | bytes 11051245 | solution.py:143
  107.6 36.7 %while.105 = (s32[]{:T(128)}, f32[512,4,64]{0,2,1:T(8,128)}, f32[2048,256]{0,1:T(8,128)}, f32[2048,256]{0,1:T(8,128)}, s32[3]{0:T(128)S(1)}, /*index=5*/bf16[204...) while((s32[]{:T(128)}, f32[512,4,64]{0,2,1:T(8,128)}, ...), condition=%wide.region_19.20_spmd.clone, body=%wide.region_18.19_spmd.clone.sunk | while | flops 685244416 | bytes 32006468 | solution.py:182
  144.3 14.1 %while.102 = (s32[]{:T(128)}, f32[4,512,1]{1,0,2:T(4,128)S(1)}, f32[4,512,1]{1,0,2:T(4,128)S(1)}, s32[3]{0:T(128)S(1)}, s32[]{:T(128)}, /*index=5*/bf16[2048,256...) while((s32[]{:T(128)}, f32[4,512,1]{1,0,2:T(4,128)S(1)}, ...), condition=%wide.region_11.12_spmd.clone, body=%wide.region_8.0_spmd.clone.sunk | while | flops 143403008 | bytes 10330334 | solution.py:95
  158.4 15.4 %while.106 = (s32[]{:T(128)}, f32[4,512,1]{1,2,0:T(1,128)S(1)}, s32[3]{0:T(128)S(1)}, s32[]{:T(128)}, bf16[2048,256]{0,1:T(8,128)(2,1)S(1)}, /*index=5*/bf16[512...) while((s32[]{:T(128)}, f32[4,512,1]{1,2,0:T(1,128)S(1)}, ...), condition=%wide.region_22.23_spmd.clone, body=%wide.region_20.0_spmd.clone.sunk | while | flops 275515392 | bytes 11051245 | solution.py:143
  173.9 30.8 %while.107 = (s32[]{:T(128)}, f32[512,4,64]{0,2,1:T(8,128)S(1)}, f32[2048,256]{0,1:T(8,128)}, f32[2048,256]{0,1:T(8,128)}, s32[3]{0:T(128)S(1)}, /*index=5*/bf16...) while((s32[]{:T(128)}, f32[512,4,64]{0,2,1:T(8,128)S(1)}, ...), condition=%wide.region_24.25_spmd.clone, body=%wide.region_23.24_spmd.clone.sunk | while | flops 685244416 | bytes 27812108 | solution.py:182
  207.0 6.6 fusion.115
  216.5 19.6 %while.101 = (s32[]{:T(128)}, f32[512,4,64]{0,2,1:T(8,128)}, s32[3]{0:T(128)S(1)}, bf16[2048,256]{0,1:T(8,128)(2,1)S(1)}, s32[]{:T(128)}, /*index=5*/bf16[2048,2...) while((s32[]{:T(128)}, f32[512,4,64]{0,2,1:T(8,128)}, ...), condition=%wide.region_7.8_spmd.clone, body=%wide.region_6.7_spmd.clone.sunk | while | flops 274726912 | bytes 3416293 | solution.py:112
  225.8 3.8 fusion.257
  232.3 3.8 fusion.257
  237.9 19.4 %while.103 = (s32[]{:T(128)}, f32[512,4,64]{0,2,1:T(8,128)}, s32[3]{0:T(128)S(1)}, bf16[2048,256]{0,1:T(8,128)(2,1)S(1)}, s32[]{:T(128)}, /*index=5*/bf16[2048,2...) while((s32[]{:T(128)}, f32[512,4,64]{0,2,1:T(8,128)}, ...), condition=%wide.region_13.14_spmd.clone, body=%wide.region_12.13_spmd.clone.sunk | while | flops 274726912 | bytes 3416293 | solution.py:112
  247.0 3.8 fusion.266
  253.5 3.9 fusion.266
  263.2 14.9 %convert_reduce_fusion.2 = (f32[1024]{0:T(1024)}, bf16[1024,1024]{1,0:T(8,128)(2,1)}, f32[1024,1024]{1,0:T(8,128)S(1)}) fusion(f32[1024,1024]{1,0:T(8,128)} %fusion.115, f32[1024]{0:T(1024)S(1)} %copy-done.35, bf16[1024,1024]{1,0:T(8,128)(2,1)S(1)} %copy-done.10, bf16[1024,1024]{1,0:T(8,128)(2,1)} %all-gather.13.cloned.1.call-done), kind=kOutput, calls=%fused_computation.163 | convolution fusion | flops 2226125824 | bytes 14688256 | tf_op jit(solution)/shard_map/te,fe->tf/dot_general | solution.py:273
  280.6 4.4 fusion.132
  286.6 6.2 fusion.113
  301.5 4.9 fusion.109
  306.5 5.0 fusion.129
  311.5 4.4 fusion.130
  323.9 22.3 %reduce-scatter.17.cloned.1.call-done = f32[1024,256]{1,0:T(8,128)} async-done(((f32[1024,1024]{1,0:T(8,128)}), f32[1024,256]{1,0:T(8,128)}) %reduce-scatter.17.cloned.1.call-update) | async-done | bytes 1048592 | tf_op jit(solution)/shard_map/reduce_scatter | solution.py:338
  346.2 46.9 %reduce-scatter.15.cloned.1.call-done = f32[256,1024]{1,0:T(8,128)} async-done(((f32[1024,1024]{1,0:T(8,128)}), f32[256,1024]{1,0:T(8,128)}) %reduce-scatter.15.cloned.1.call-update) | async-done | bytes 1048592 | tf_op jit(solution)/shard_map/reduce_scatter | solution.py:337
  393.1 40.7 %reduce-scatter.11.cloned.1.call-done = f32[256,3,256]{2,0,1:T(8,128)} async-done(((f32[1024,3,256]{2,0,1:T(8,128)}), f32[256,3,256]{2,0,1:T(8,128)}) %reduce-scatter.11.cloned.1.call-update) | async-done | bytes 786448 | tf_op jit(solution)/shard_map/reduce_scatter | solution.py:335
  433.8 430.2 %all-reduce.6.cloned.1.call-done = (f32[1024,1024]{1,0:T(8,128)}, f32[1024,1024]{1,0:T(8,128)}, f32[1024,1024]{1,0:T(8,128)}) async-done(((f32[1024,1024]{1,0:T(8,128)}, f32[1024,1024]{1,0:T(8,128)}, f32[1024,1024]{1,0:T(8,128)}), (f32[1024,1024]{1,0:T(8,128)}, f32[1024,1024]{1,0:T(8,128)}, f32[1024,1024]{1,0:T(8,128)})) %all-reduce.6.cloned.1.call-update) | async-done | bytes 12582928 | tf_op jit(solution)/shard_map/psum | solution.py:265
  864.0 5.3 fusion.120
  870.0 3.9 fusion.95
  874.0 5.1 convert_reduce_fusion.1
  879.1 25.5 %all-reduce = (f32[3,256]{1,0:T(4,128)}, f32[1024]{0:T(1024)S(1)}, f32[1024]{0:T(1024)}, f32[1024]{0:T(1024)}, f32[1024]{0:T(1024)}, /*index=5*/f32[1024]{0:T(1024)}, f32[1024]{0:T(1024)}) all-reduce(f32[3,256]{1,0:T(4,128)S(1)} %convert_reduce_fusion.3, ...), channel_id=1, replica_groups=mesh['fsdp'=4,'context'=2,'tensor'=4] {'fsdp','context'}, use_global_device_ids=true, to_apply=%region_36.37 | all-reduce | flops 6912 | bytes 55296 | tf_op jit(solution)/shard_map/psum | solution.py:328
  904.6 48.4 %all-reduce.8.cloned.1.call-done = (f32[256,3,256]{2,0,1:T(8,128)}, f32[256,256]{1,0:T(8,128)}, f32[256,1024]{1,0:T(8,128)}, f32[1024,256]{1,0:T(8,128)}) async-done(((f32[256,3,256]{2,0,1:T(8,128)}, f32[256,256]{1,0:T(8,128)}, f32[256,1024]{1,0:T(8,128)}, f32[1024,256]{1,0:T(8,128)}), (f32[256,3,256]{2,0,1:T(8,128)}, f32[256,256]{1,0:T(8,128)}, f32[256,1024]{1,0:T(8,128)}, ...) | async-done | bytes 3145744 | tf_op jit(solution)/shard_map/psum | solution.py:340
  (361 shorter events, 173.4 us)
Async XLA Ops:
  7.2 25.6 %copy-start.30 = (f32[1024]{0:T(1024)S(1)}, f32[1024]{0:T(1024)}, u32[]{:S(2)}) copy-start(f32[1024]{0:T(1024)} %param.46) | copy-start | bytes 12292
  7.2 25.6 %copy-start.45 = (f32[1024]{0:T(1024)S(1)}, f32[1024]{0:T(1024)}, u32[]{:S(2)}) copy-start(f32[1024]{0:T(1024)} %param.47) | copy-start | bytes 12292
  7.2 25.5 %copy-start.43 = (f32[3,256]{1,0:T(4,128)S(1)}, f32[3,256]{1,0:T(4,128)}, u32[]{:S(2)}) copy-start(f32[3,256]{1,0:T(4,128)} %param.39) | copy-start | bytes 9220
  7.2 25.5 %all-gather.7.cloned.1.call-start = ((), (), s32[]{:S(2)}) async-start(), calls=%async_computation.6 | async-start | bytes 1966080 | tf_op jit(solution)/shard_map/all_gather | solution.py:212
  9.3 50.4 %all-gather.9.cloned.1.call-start = ((), (), s32[]{:S(2)}) async-start(), calls=%async_computation.7 | async-start | bytes 1572864 | tf_op jit(solution)/shard_map/all_gather | solution.py:237
  12.1 24.1 %copy-start.26 = (f32[1024]{0:T(1024)}, f32[1024]{0:T(1024)S(1)}, u32[]{:S(2)}) copy-start(f32[1024]{0:T(1024)S(1)} %broadcast_multiply_fusion) | copy-start | bytes 12292
  13.4 22.8 %copy-start.33 = (f32[1024]{0:T(1024)}, f32[1024]{0:T(1024)S(1)}, u32[]{:S(2)}) copy-start(f32[1024]{0:T(1024)S(1)} %fusion.112) | copy-start | bytes 12292
  13.6 23.0 %copy-start.23 = (f32[1024,8]{0,1:T(8,128)}, f32[1024,8]{0,1:T(8,128)S(1)}, u32[]{:S(2)}) copy-start(f32[1024,8]{0,1:T(8,128)S(1)} %get-tuple-element.940) | copy-start | bytes 98308
  13.6 23.0 %copy-start.24 = (f32[1024,8]{0,1:T(8,128)}, f32[1024,8]{0,1:T(8,128)S(1)}, u32[]{:S(2)}) copy-start(f32[1024,8]{0,1:T(8,128)S(1)} %get-tuple-element.941) | copy-start | bytes 98308
  36.5 12.6 %copy-start.9 = (bf16[1024,1024]{1,0:T(8,128)(2,1)S(1)}, bf16[1024,1024]{1,0:T(8,128)(2,1)}, u32[]{:S(2)}) copy-start(bf16[1024,1024]{1,0:T(8,128)(2,1)} %param.35) | copy-start | bytes 6291460
  38.2 45.0 %all-gather.15.cloned.1.call-start = ((), (), s32[]{:S(2)}) async-start(), calls=%async_computation.16 | async-start | bytes 1572864 | tf_op jit(solution)/shard_map/all_gather | solution.py:238
  40.5 166.4 %all-gather.11.cloned.1.call-start = ((), (), s32[]{:S(2)}) async-start(), calls=%async_computation.8 | async-start | bytes 2621440 | tf_op jit(solution)/shard_map/all_gather | solution.py:214
  41.1 222.1 %all-gather.13.cloned.1.call-start = ((), (), s32[]{:S(2)}) async-start(), calls=%async_computation.9 | async-start | bytes 2621440 | tf_op jit(solution)/shard_map/all_gather | solution.py:215
  41.7 253.3 %reduce-scatter.7.cloned.1.call-start = ((), (), s32[]{:S(2)}) async-start(), calls=%async_computation.10 | async-start | bytes 3145728 | tf_op jit(solution)/shard_map/reduce_scatter | solution.py:303
  173.9 33.1 %copy-start.27 = (f32[1024]{0:T(1024)S(1)}, f32[1024]{0:T(1024)}, u32[]{:S(2)}) copy-start(f32[1024]{0:T(1024)} %copy-done.26) | copy-start | bytes 12292
  173.9 33.1 %copy-start.32 = (f32[1024]{0:T(1024)S(1)}, f32[1024]{0:T(1024)}, u32[]{:S(2)}) copy-start(f32[1024]{0:T(1024)} %param.48) | copy-start | bytes 12292
  173.9 33.1 %copy-start.34 = (f32[1024]{0:T(1024)S(1)}, f32[1024]{0:T(1024)}, u32[]{:S(2)}) copy-start(f32[1024]{0:T(1024)} %copy-done.33) | copy-start | bytes 12292
  173.9 33.1 %copy-start.44 = (f32[1024]{0:T(1024)S(1)}, f32[1024]{0:T(1024)}, u32[]{:S(2)}) copy-start(f32[1024]{0:T(1024)} %param.49) | copy-start | bytes 12292
  204.7 95.5 %reduce-scatter.9.cloned.1.call-start = ((), (), s32[]{:S(2)}) async-start(), calls=%async_computation.11 | async-start | bytes 3145728 | tf_op jit(solution)/shard_map/reduce_scatter | solution.py:304
  216.5 107.5 %reduce-scatter.13.cloned.1.call-start = ((), (), s32[]{:S(2)}) async-start(), calls=%async_computation.13 | async-start | bytes 1310720 | tf_op jit(solution)/shard_map/reduce_scatter | solution.py:336
  257.4 5.8 copy-start.35
  259.6 18.5 %copy-start.12 = (bf16[1024,4,64]{0,2,1:T(8,128)(2,1)}, bf16[1024,4,64]{0,2,1:T(8,128)(2,1)S(1)}, u32[]{:S(2)}) copy-start(bf16[1024,4,64]{0,2,1:T(8,128)(2,1)S(1)} %pad_maximum_fusion.3) | copy-start | bytes 1572868
  263.1 83.1 %reduce-scatter.17.cloned.1.call-start = ((), (), s32[]{:S(2)}) async-start(), calls=%async_computation.15 | async-start | bytes 5242880 | tf_op jit(solution)/shard_map/reduce_scatter | solution.py:338
  263.2 14.9 %copy-start.14 = (f32[1024,1024]{1,0:T(8,128)S(1)}, f32[1024,1024]{1,0:T(8,128)}, u32[]{:S(2)}) copy-start(f32[1024,1024]{1,0:T(8,128)} %fusion.115) | copy-start | bytes 12582916
  285.0 108.1 %reduce-scatter.15.cloned.1.call-start = ((), (), s32[]{:S(2)}) async-start(), calls=%async_computation.14 | async-start | bytes 5242880 | tf_op jit(solution)/shard_map/reduce_scatter | solution.py:337
  292.8 141.0 %reduce-scatter.11.cloned.1.call-start = ((), (), s32[]{:S(2)}) async-start(), calls=%async_computation.12 | async-start | bytes 3932160 | tf_op jit(solution)/shard_map/reduce_scatter | solution.py:335
  294.9 6.6 copy-start.31
  306.4 557.6 %all-reduce.6.cloned.1.call-start = ((), (), s32[]{:S(2)}) async-start(), calls=%async_computation.17 | async-start | bytes 25165824 | tf_op jit(solution)/shard_map/psum | solution.py:265
  322.4 630.5 %all-reduce.8.cloned.1.call-start = ((), (), s32[]{:S(2)}) async-start(), calls=%async_computation.18 | async-start | bytes 6291456 | tf_op jit(solution)/shard_map/psum | solution.py:340
  864.0 5.9 copy-start.5
  904.6 56.0 %copy-start.37 = (f32[1024]{0:T(1024)}, f32[1024]{0:T(1024)S(1)}, u32[]{:S(2)}) copy-start(f32[1024]{0:T(1024)S(1)} %get-tuple-element.1765) | copy-start | bytes 12292
  953.0 6.6 copy-start.22
  (32 other events, 110.1 us)
Sparse Core Ops, SparseCore 0:
  10.2 22.5 all-gather.6
  38.4 21.3 all-gather.8
  61.8 21.3 all-gather.14
  84.6 22.5 all-gather.10
  108.6 22.8 all-gather.12
  204.9 31.8 reduce-scatter.6
  239.1 31.8 reduce-scatter.8
  274.0 24.8 reduce-scatter.12
  301.7 44.5 reduce-scatter.16
  348.6 44.4 reduce-scatter.14
  395.8 37.9 reduce-scatter.10
  436.5 427.4 all-reduce.5
  866.5 86.4 all-reduce.7
where the time goes:
time: 974 us; the launch traced here: 967 us
  waiting for transfers between devices  623 us (64%)
  matrix products  142 us (15%)
  other arithmetic  52.7 us (5%)
  local copies, waits for them, and re-layouts  52 us (5%)
  loops' own time  48.7 us (5%)
  blocking collectives  32.7 us (3%)
  between operations  14.9 us (2%)
    psum x1, waiting for transfers between devices, body(): summed = lax.psum(partial_out, 'tensor')  430 us
    psum x1, waiting for transfers between devices, body(): shards = lax.psum((shards[0], shards[1], shards[2], shards[3]), 'context')  48.4 us
    reduce_scatter x1, waiting for transfers between devices, body(): lax.psum_scatter(up_grad, 'fsdp', scatter_dimension=0, tiled=True)  46.9 us
    reduce_scatter x1, waiting for transfers between devices, body(): lax.psum_scatter(project_grad, 'fsdp', scatter_dimension=0, tiled=True)  40.7 us
    psum x1, blocking collectives, body(): lax.psum((project_bias_grad, bias_total, up_bias_grad, gain_one, shift_on...  25.5 us
    dot_general x6, matrix products, second_pass(): jnp.einsum('hqk,khd->qhd', probability, value_block, preferred_element_ty...  22.6 us
    reduce_scatter x1, waiting for transfers between devices, body(): lax.psum_scatter(down_grad, 'fsdp', scatter_dimension=1, tiled=True)  22.3 us
  transfers between devices with their start and end apart: 13, of which 8 were waited for; matrix products, arithmetic and copies ran while one was open for 23% of the time, Pallas kernels for 0%

commit v1 on v0

v1 whole, which is shorter than its diff:
```python
from functools import partial

import jax
import jax.numpy as jnp
from jax import lax
from jax.experimental import pallas as pl
from jax.experimental.pallas import tpu as pltpu
from jax.sharding import PartitionSpec as P

HD = 64
ROT = 16
BLK = 512
PAIR = 2 * HD

epsilon = 1e-05
masked = -1e30
bf16 = jnp.bfloat16
f32 = jnp.float32
scale2 = HD ** (-0.5) * 1.4426950408889634
NT = (((1,), (1,)), ((), ()))
NN = (((1,), (0,)), ((), ()))
TN = (((0,), (0,)), ((), ()))


def dot(a, b, dims):
    return lax.dot_general(a, b, dims, preferred_element_type=f32)


def params(**kw):
    return pltpu.CompilerParams(vmem_limit_bytes=56 * 1024 * 1024, **kw)


def whole(shape):
    return pl.BlockSpec(shape, lambda *_: (0,) * len(shape))


smem = pl.BlockSpec(memory_space=pltpu.SMEM)


def norm_rows(x):
    mean = jnp.mean(x, axis=-1, keepdims=True)
    centered = x - mean
    variance = jnp.mean(centered * centered, axis=-1, keepdims=True)
    factor = lax.rsqrt(variance + epsilon)
    return centered * factor, factor


def rotate_lanes(x, cos, low_sin, high_sin, sign):
    left = pltpu.roll(x, PAIR - ROT // 2, 1)
    right = pltpu.roll(x, ROT // 2, 1)
    return x * cos + sign * (left * low_sin + right * high_sin)


def columns(index, width):
    return pl.ds(pl.multiple_of(index * width, width), width)


def project_kernel(ids, n1, w0, w1, w2, w3, bias, cos, lows, highs, q0, q1, kv0, kv1):
    weights = (w0, w1, w2, w3)
    width = w0.shape[2]
    depth = w0.shape[1]
    outs = ((q0, q1), (kv0, kv1))
    for part in range(3):
        total = bias[part : part + 1, :] + jnp.zeros((n1.shape[0], width), f32)
        for piece in range(4):
            total += dot(n1[:, columns(ids[piece], depth)], weights[piece][part], NN)
        for pair in range(2):
            half = total[:, pair * PAIR : (pair + 1) * PAIR]
            if part < 2:
                half = rotate_lanes(half, cos[...], lows[...], highs[...], 1.0)
            if part == 0:
                outs[0][pair][...] = half.astype(bf16)
            else:
                outs[1][pair][:, (part - 1) * PAIR : part * PAIR] = half.astype(bf16)


def project(ids, n1, weights, bias, tables, tile=256):
    rows = n1.shape[0]
    row = lambda w: pl.BlockSpec((tile, w), lambda i: (i, 0))
    return pl.pallas_call(
        project_kernel,
        grid=(rows // tile,),
        in_specs=[smem, row(n1.shape[1])]
        + [whole(w.shape) for w in weights]
        + [whole(bias.shape)]
        + [row(PAIR)] * 3,
        out_specs=[row(PAIR)] * 2 + [row(2 * PAIR)] * 2,
        out_shape=[jax.ShapeDtypeStruct((rows, PAIR), bf16)] * 2
        + [jax.ShapeDtypeStruct((rows, 2 * PAIR), bf16)] * 2,
        compiler_params=params(),
        name="project",
    )(ids, n1, *weights, bias, *tables)


def head_lanes(shape, head):
    return lax.broadcasted_iota(jnp.int32, shape, 1) // HD == head


def load_keys(kvs, kv_scr):
    start = 0
    for part in kvs:
        count = part.shape[0] // BLK
        for block in range(count):
            kv_scr[start + block] = part[block * BLK : (block + 1) * BLK, :]
        start += count


def attend_forward_kernel(slots, maxk, ids, q, *refs):
    parts = refs[: -6]
    o, lse, kv, turned, state, acc = refs[-6:]
    load_keys(parts, kv)
    for slot in range(slots):
        turned[slot] = kv[slot][:, PAIR:].T
    for block in range(q.shape[0] // BLK):
        own = ids[0] + block
        for head in range(2):
            rows = slice(head * HD, (head + 1) * HD)
            query = q[block * BLK : (block + 1) * BLK, :]
            query = jnp.where(head_lanes(query.shape, head), query, jnp.zeros_like(query))

            scores = dot(kv[own][:, :PAIR], query, NT) * scale2
            keep = lax.broadcasted_iota(jnp.int32, scores.shape, 0) <= lax.broadcasted_iota(
                jnp.int32, scores.shape, 1
            )
            scores = jnp.where(keep, scores, masked)
            top = jnp.max(scores, axis=0, keepdims=True)
            weight = jnp.exp2(scores - top)
            state[0:1, :] = top
            state[1:2, :] = jnp.sum(weight, axis=0, keepdims=True)
            acc[rows, :] = dot(turned[own][rows, :], weight.astype(bf16), NN)

            def entry(step, unused):
                slot = ids[2 + block * maxk + step]

                @pl.when((slot >= 0) & (slot != own))
                def _():
                    scores = dot(kv[slot][:, :PAIR], query, NT) * scale2
                    old = state[0:1, :]
                    top = jnp.maximum(old, jnp.max(scores, axis=0, keepdims=True))
                    weight = jnp.exp2(scores - top)
                    shrink = jnp.exp2(old - top)
                    state[0:1, :] = top
                    state[1:2, :] = state[1:2, :] * shrink + jnp.sum(weight, axis=0, keepdims=True)
                    acc[rows, :] = acc[rows, :] * shrink + dot(
                        turned[slot][rows, :], weight.astype(bf16), NN
                    )

                return unused

            lax.fori_loop(0, maxk, entry, 0)
            line = block * 2 + head
            lse[line : line + 1, :] = state[0:1, :] + jnp.log2(state[1:2, :])
            acc[rows, :] = acc[rows, :] * (1.0 / state[1:2, :])
        o[block * BLK : (block + 1) * BLK, :] = acc[...].T


def attend_forward(ids, maxk, q, kvs):
    slots = sum(part.shape[0] for part in kvs) // BLK
    rows = q.shape[0]
    return pl.pallas_call(
        partial(attend_forward_kernel, slots, maxk),
        grid=(),
        in_specs=[smem] + [pl.BlockSpec(memory_space=pltpu.VMEM)] * (1 + len(kvs)),
        out_specs=[pl.BlockSpec(memory_space=pltpu.VMEM)] * 2,
        out_shape=[
            jax.ShapeDtypeStruct((rows, PAIR), f32),
            jax.ShapeDtypeStruct((8, BLK), f32),
        ],
        scratch_shapes=[
            pltpu.VMEM((slots, BLK, 2 * PAIR), bf16),
            pltpu.VMEM((slots, PAIR, BLK), bf16),
            pltpu.VMEM((8, BLK), f32),
            pltpu.VMEM((PAIR, BLK), f32),
        ],
        compiler_params=params(),
        name="attend_forward",
    )(ids, q, *kvs)


def attend_backward_kernel(slots, maxk, split, ids, q, g, o, lse, cos, lows, highs, *refs):
    outs = 2 if split else 1
    parts = refs[: -5 - outs]
    grads = refs[-5 - outs : -5]
    qg, kv, turned, acc, total = refs[-5:]
    load_keys(parts, kv)
    for slot in range(slots):
        turned[slot] = kv[slot][:, :PAIR].T
    total[...] = jnp.zeros_like(total)
    pick = (
        lax.broadcasted_iota(jnp.int32, (8, PAIR), 1) // HD
        == lax.broadcasted_iota(jnp.int32, (8, PAIR), 0)
    ).astype(f32)
    for block in range(q.shape[0] // BLK):
        own = ids[0] + block
        span = slice(block * BLK, (block + 1) * BLK)
        deltas = lax.dot_general(
            pick,
            o[span, :] * g[span, :].astype(f32),
            NT,
            preferred_element_type=f32,
            precision=lax.Precision.HIGHEST,
        )
        for head in range(2):
            rows = slice(head * HD, (head + 1) * HD)
            lanes = head_lanes((BLK, PAIR), head)
            query = q[span, :]
            query = jnp.where(lanes, query, jnp.zeros_like(query))
            grad = g[span, :]
            grad = jnp.where(lanes, grad, jnp.zeros_like(grad))
            line = block * 2 + head
            log_sum = lse[line : line + 1, :]
            delta = deltas[head : head + 1, :]

            def tile(slot, keep):
                scores = dot(kv[slot][:, :PAIR], query, NT) * scale2
                prob = jnp.exp2(scores - log_sum)
                if keep is not None:
                    prob = jnp.where(keep, prob, 0.0)
                prob_grad = dot(kv[slot][:, PAIR:], grad, NT)
                score_grad = (prob * (prob_grad - delta)).astype(bf16)
                total[slot, :, PAIR:] += dot(prob.astype(bf16), grad, NN)
                total[slot, :, :PAIR] += dot(score_grad, query, NN)
                return dot(turned[slot][rows, :], score_grad, NN)

            keep = lax.broadcasted_iota(jnp.int32, (BLK, BLK), 0) <= lax.broadcasted_iota(
                jnp.int32, (BLK, BLK), 1
            )
            acc[rows, :] = tile(own, keep)

            def entry(step, unused):
                slot = ids[2 + block * maxk + step]

                @pl.when((slot >= 0) & (slot != own))
                def _():
                    acc[rows, :] += tile(slot, None)

                return unused

            lax.fori_loop(0, maxk, entry, 0)
        grad_q = acc[...].T * (HD ** (-0.5))
        qg[span, :] = rotate_lanes(
            grad_q, cos[span, :], lows[span, :], highs[span, :], -1.0
        ).astype(bf16)
    start = 0
    for out in grads:
        count = out.shape[0] // BLK
        for block in range(count):
            out[block * BLK : (block + 1) * BLK, :] = total[start + block].astype(out.dtype)
        start += count


def attend_backward(ids, maxk, q, g, o, lse, tables, kvs):
    slots = sum(part.shape[0] for part in kvs) // BLK
    rows = q.shape[0]
    split = len(kvs) == 2
    shapes = [jax.ShapeDtypeStruct(kvs[0].shape, f32 if split else bf16)]
    if split:
        shapes.append(jax.ShapeDtypeStruct(kvs[1].shape, bf16))
    shapes.append(jax.ShapeDtypeStruct((rows, PAIR), bf16))
    vmem = pl.BlockSpec(memory_space=pltpu.VMEM)
    return pl.pallas_call(
        partial(attend_backward_kernel, slots, maxk, split),
        grid=(),
        in_specs=[smem] + [vmem] * (7 + len(kvs)),
        out_specs=[vmem] * len(shapes),
        out_shape=shapes,
        scratch_shapes=[
            pltpu.VMEM((slots, BLK, 2 * PAIR), bf16),
            pltpu.VMEM((slots, PAIR, BLK), bf16),
            pltpu.VMEM((PAIR, BLK), f32),
            pltpu.VMEM((slots, BLK, 2 * PAIR), f32),
        ],
        compiler_params=params(),
        name="attend_backward",
    )(ids, q, g, o, lse, *tables, *kvs)


def mlp_kernel(
    ids, x, cot, gain, shift, up_bias, u0, u1, u2, u3, d0, d1, d2, d3, c0, c1, c2, c3,
    n2, act, hid_grad, mlp, e2, g0, g1, up_sum, norm_sums,
):
    ups, downs, denses = (u0, u1, u2, u3), (d0, d1, d2, d3), (c0, c1, c2, c3)
    depth = u0.shape[0]
    step = pl.program_id(0)

    @pl.when(step == 0)
    def _():
        up_sum[...] = jnp.zeros_like(up_sum)
        norm_sums[...] = jnp.zeros_like(norm_sums)

    normal, _ = norm_rows(x[...].astype(f32))
    n2[...] = (normal * gain[...] + shift[...]).astype(bf16)
    hidden = up_bias[...] + jnp.zeros((x.shape[0], u0.shape[1]), f32)
    back = jnp.zeros((x.shape[0], u0.shape[1]), f32)
    context_grad = jnp.zeros((x.shape[0], c0.shape[0]), f32)
    for piece in range(4):
        where = columns(ids[piece], depth)
        hidden += dot(n2[:, where], ups[piece][...], NN)
        back += dot(cot[:, where], downs[piece][...], NT)
        context_grad += dot(cot[:, where], denses[piece][...], NT)
    g0[...] = context_grad[:, :PAIR].astype(bf16)
    g1[...] = context_grad[:, PAIR:].astype(bf16)
    cdf = 0.5 + 0.5 * lax.erf(hidden * (2.0 ** -0.5))
    pdf = jnp.exp(hidden * hidden * -0.5) * 0.3989422804014327
    act[...] = (hidden * cdf).astype(bf16)
    low = (back * (cdf + hidden * pdf)).astype(bf16)
    hid_grad[...] = low
    up_sum[...] += jnp.sum(low.astype(f32), axis=0, keepdims=True)
    for piece in range(4):
        where = columns(ids[piece], depth)
        mlp[:, where] = dot(act[...], downs[piece][...], NN)
        e2[:, where] = dot(low, ups[piece][...], NT)
    grad = e2[...]
    norm_sums[0:1, :] += jnp.sum(grad * normal, axis=0, keepdims=True)
    norm_sums[1:2, :] += jnp.sum(grad, axis=0, keepdims=True)
    e2[...] = grad * gain[...]


def mlp_all(ids, x, cot, gain, shift, up_bias, ups, downs, denses, tile=256):
    rows, width = x.shape
    units = up_bias.shape[1]
    row = lambda w: pl.BlockSpec((tile, w), lambda i: (i, 0))
    s = jax.ShapeDtypeStruct
    return pl.pallas_call(
        mlp_kernel,
        grid=(rows // tile,),
        in_specs=[smem, row(width), row(width)]
        + [whole(a.shape) for a in (gain, shift, up_bias, *ups, *downs, *denses)],
        out_specs=[
            row(width), row(units), row(units), row(width), row(width), row(PAIR), row(PAIR),
            whole((1, units)), whole((8, width)),
        ],
        out_shape=[
            s((rows, width), bf16), s((rows, units), bf16), s((rows, units), bf16),
            s((rows, width), f32), s((rows, width), f32), s((rows, PAIR), bf16),
            s((rows, PAIR), bf16), s((1, units), f32), s((8, width), f32),
        ],
        compiler_params=params(),
        name="mlp_all",
    )(ids, x, cot, gain, shift, up_bias, *ups, *downs, *denses)


def output_kernel(ids, o0, o1, mlp, c0, c1, c2, c3, out, ctx):
    width = c0.shape[1]
    ctx[:, :PAIR] = o0[...].astype(bf16)
    ctx[:, PAIR:] = o1[...].astype(bf16)
    for piece, weight in enumerate((c0, c1, c2, c3)):
        where = columns(ids[piece], width)
        out[:, where] = (mlp[:, where] + dot(ctx[...], weight[...], NN)).astype(bf16)


def output_part(ids, o0, o1, mlp, denses, tile=256):
    rows, width = mlp.shape
    row = lambda w: pl.BlockSpec((tile, w), lambda i: (i, 0))
    return pl.pallas_call(
        output_kernel,
        grid=(rows // tile,),
        in_specs=[smem, row(PAIR), row(PAIR), row(width)] + [whole(a.shape) for a in denses],
        out_specs=[row(width), row(2 * PAIR)],
        out_shape=[
            jax.ShapeDtypeStruct((rows, width), bf16),
            jax.ShapeDtypeStruct((rows, 2 * PAIR), bf16),
        ],
        compiler_params=params(),
        name="output_part",
    )(ids, o0, o1, mlp, *denses)


def input_grad_kernel(
    split, ids, x, e2, gain, qg0, qg1, cos, lows, highs, w0, w1, w2, w3, *refs
):
    grads, (pg, e, norm_sums, bias_sum, first) = refs[:-5], refs[-5:]
    weights = (w0, w1, w2, w3)
    depth = w0.shape[1]
    width = w0.shape[2]

    @pl.when(pl.program_id(0) == 0)
    def _():
        norm_sums[...] = jnp.zeros_like(norm_sums)
        bias_sum[...] = jnp.zeros_like(bias_sum)

    pg[:, 0:PAIR] = qg0[...]
    pg[:, PAIR : 2 * PAIR] = qg1[...]
    for pair in range(2):
        if split:
            own, other = grads[2 * pair : 2 * pair + 2]
            grad = own[...] + other[...].astype(f32)
        else:
            grad = grads[pair][...].astype(f32)
        key = rotate_lanes(
            grad[:, :PAIR] * (HD ** (-0.5)), cos[...], lows[...], highs[...], -1.0
        )
        at = width + pair * PAIR
        pg[:, at : at + PAIR] = key.astype(bf16)
        pg[:, at + width : at + width + PAIR] = grad[:, PAIR:].astype(bf16)
    bias_sum[...] += jnp.sum(pg[...].astype(f32), axis=0, keepdims=True)
    normal, _ = norm_rows(x[...].astype(f32))
    for piece in range(4):
        where = columns(ids[piece], depth)
        total = dot(pg[:, :width], weights[piece][0], NT)
        total += dot(pg[:, width : 2 * width], weights[piece][1], NT)
        total += dot(pg[:, 2 * width :], weights[piece][2], NT)
        first[:, where] = total
    grad = first[...]
    e[...] = (grad * gain[...] + e2[...]).astype(bf16)
    norm_sums[0:1, :] += jnp.sum(grad * normal, axis=0, keepdims=True)
    norm_sums[1:2, :] += jnp.sum(grad, axis=0, keepdims=True)


def input_grad(ids, x, e2, gain, qgs, tables, weights, grads, split, tile=256):
    rows, width = x.shape
    row = lambda w: pl.BlockSpec((tile, w), lambda i: (i, 0))
    s = jax.ShapeDtypeStruct
    units = 3 * weights[0].shape[2]
    return pl.pallas_call(
        partial(input_grad_kernel, split),
        grid=(rows // tile,),
        in_specs=[smem, row(width), row(width), whole(gain.shape), row(PAIR), row(PAIR)]
        + [row(PAIR)] * 3
        + [whole(w.shape) for w in weights]
        + [row(2 * PAIR)] * len(grads),
        out_specs=[row(units), row(width), whole((8, width)), whole((1, units))],
        out_shape=[
            s((rows, units), bf16), s((rows, width), bf16), s((8, width), f32),
            s((1, units), f32),
        ],
        scratch_shapes=[pltpu.VMEM((tile, width), f32)],
        compiler_params=params(),
        name="input_grad",
    )(ids, x, e2, gain, *qgs, *tables, *weights, *grads)


def swap(values, axis, size, bit):
    pairs = [(i, i ^ bit) for i in range(size)]
    return jax.tree.map(lambda v: lax.ppermute(v, axis, pairs), values)


def sum_all(value, axes):
    for axis, size in axes:
        bit = 1
        while bit < size:
            value = value + swap(value, axis, size, bit)
            bit *= 2
    return value


def pieces_of(shard):
    first = swap(shard, "fsdp", 4, 2)
    return (shard, swap(shard, "fsdp", 4, 1), first, swap(first, "fsdp", 4, 1))


def shard_of(grad, me, context):
    core, chip = me % 2, me // 2
    grad = grad.reshape((2, 2) + grad.shape[1:])
    pick = lambda a, i, d: lax.dynamic_index_in_dim(a, i, d, keepdims=False)
    kept, sent = pick(grad, core, 1), pick(grad, 1 - core, 1)
    got = swap(sent, "fsdp", 4, 1)
    grad = (kept.astype(f32) + got.astype(f32)).astype(bf16)
    kept, sent = pick(grad, chip, 0), pick(grad, 1 - chip, 0)
    got = swap(sent, "fsdp", 4, 2)
    grad = (kept.astype(f32) + got.astype(f32)).astype(bf16)
    if context == 2:
        return grad.astype(f32) + swap(grad, "context", 2, 1).astype(f32)
    return lax.psum(grad.astype(f32), "context")


def all_sum_rows(value, finish, chunks):
    size = value.shape[0] // chunks
    place = lax.axis_index("tensor")
    middle = (place == 1) | (place == 2)
    done = []
    for index in range(chunks):
        part = value[index * size : (index + 1) * size]
        got = lax.ppermute(part, "tensor", [(0, 1), (3, 2)])
        part = (part.astype(f32) + got.astype(f32)).astype(bf16)
        got = lax.ppermute(part, "tensor", [(1, 2), (2, 1)])
        final = finish(part.astype(f32) + got.astype(f32), index * size, size)
        got = lax.ppermute(final, "tensor", [(1, 0), (2, 3)])
        done.append(jnp.where(middle, final, got))
    return jnp.concatenate(done, axis=0)


def rotation_tables(positions):
    lane = jnp.arange(PAIR, dtype=jnp.int32) % HD
    half = ROT // 2
    frequency = jnp.exp(
        -jnp.log(10000.0) * (lane % half).astype(f32) * 2.0 / ROT
    )
    angle = positions.astype(f32)[:, None] * frequency[None, :]
    cos = jnp.where(lane < ROT, jnp.cos(angle), 1.0)
    sin = jnp.sin(angle)
    return (
        cos,
        jnp.where(lane < half, -sin, 0.0),
        jnp.where((lane >= half) & (lane < ROT), sin, 0.0),
    )


def body(
    contexts,
    tokens,
    cotangent,
    segments,
    positions,
    parents,
    block_lists,
    project_weight,
    project_bias,
    dense_weight,
    dense_bias,
    up_weight,
    up_bias,
    down_weight,
    down_bias,
    first_gain,
    first_shift,
    second_gain,
    second_shift,
):
    rows, width = tokens.shape
    blocks = rows // BLK
    maxk = block_lists.shape[1]
    me = lax.axis_index("fsdp")
    place = lax.axis_index("context")
    order = jnp.stack([me, me ^ 1, me ^ 2, me ^ 3]).astype(jnp.int32)
    split = contexts == 2
    slots = contexts * blocks
    first_slot = place * blocks
    if split:
        lists = jnp.where(block_lists >= 0, (block_lists - first_slot) % slots, -1)
        base = jnp.zeros((), jnp.int32)
    else:
        lists, base = block_lists, first_slot
    ids = jnp.concatenate(
        [jnp.stack([base, base]).astype(jnp.int32), lists.reshape(-1).astype(jnp.int32)]
    )

    projects = pieces_of(jnp.transpose(project_weight, (1, 0, 2)))
    denses = pieces_of(dense_weight)
    ups = pieces_of(up_weight)
    downs = pieces_of(down_weight)

    inputs = tokens.astype(f32)
    normal, factor = norm_rows(inputs)
    normed_one = (normal * first_gain + first_shift).astype(bf16)
    tables = rotation_tables(positions)
    q0, q1, kv0, kv1 = project(order, normed_one, projects, project_bias, tables)
    if split:
        keys = [(kv, swap(kv, "context", 2, 1)) for kv in (kv0, kv1)]
    else:
        keys = [(lax.all_gather(kv, "context", axis=0, tiled=True),) for kv in (kv0, kv1)]

    (
        normed_two, activated, hidden_grad, mlp_out, e2, g0, g1, up_sum, sums_two,
    ) = mlp_all(
        order, tokens, cotangent, second_gain[None], second_shift[None], up_bias[None],
        ups, downs, denses,
    )
    o0, lse0 = attend_forward(ids, maxk, q0, keys[0])
    o1, lse1 = attend_forward(ids, maxk, q1, keys[1])
    partial_out, context_low = output_part(order, o0, o1, mlp_out, denses)
    summed = lax.psum_scatter(partial_out, "tensor", scatter_dimension=0, tiled=True)
    quarter = summed.shape[0]
    mine = lax.dynamic_slice_in_dim(tokens, lax.axis_index("tensor") * quarter, quarter, 0)
    layer_out = (mine.astype(f32) + summed.astype(f32) + dense_bias + down_bias).astype(bf16)
    layer_out = lax.all_gather(layer_out, "tensor", axis=0, tiled=True)

    back0 = attend_backward(ids, maxk, q0, g0, o0, lse0, tables, keys[0])
    back1 = attend_backward(ids, maxk, q1, g1, o1, lse1, tables, keys[1])
    if split:
        grads = []
        for own, other, _ in (back0, back1):
            grads += [own, swap(other, "context", 2, 1)]
    else:
        grads = [
            lax.psum_scatter(whole_grad, "context", scatter_dimension=0, tiled=True)
            for whole_grad, _ in (back0, back1)
        ]
    projected_grad, e, sums_one, project_sum = input_grad(
        order, tokens, e2, first_gain[None], (back0[-1], back1[-1]), tables, projects, grads, split
    )

    upstream = cotangent.astype(f32)

    def finish(total, start, size):
        n = normal[start : start + size]
        r = factor[start : start + size]
        mean_e = jnp.mean(total, axis=-1, keepdims=True)
        mean_en = jnp.mean(total * n, axis=-1, keepdims=True)
        result = upstream[start : start + size] + r * (total - mean_e - n * mean_en)
        return result.astype(bf16)

    tokens_grad = all_sum_rows(e, finish, 4)

    product = lambda a, b: lax.dot_general(a, b, TN, preferred_element_type=f32).astype(bf16)
    up_grad = product(normed_two, hidden_grad).reshape(4, width // 4, -1)
    down_grad = product(activated, cotangent).reshape(-1, 4, width // 4).transpose(1, 0, 2)
    dense_grad = product(context_low, cotangent).reshape(-1, 4, width // 4).transpose(1, 0, 2)
    project_grad = product(normed_one, projected_grad).reshape(4, width // 4, -1)
    up_grad = shard_of(up_grad, me, contexts)
    down_grad = shard_of(down_grad, me, contexts)
    dense_grad = shard_of(dense_grad, me, contexts)
    project_grad = shard_of(project_grad, me, contexts)

    bias_total = jnp.sum(upstream, axis=0, keepdims=True)
    data = (("fsdp", 4), ("context", contexts))
    everything = sum_all(
        jnp.concatenate([up_sum, project_sum, bias_total, sums_one[:1], sums_one[1:2], sums_two[:1], sums_two[1:2]], axis=1),
        data,
    )
    units = up_bias.shape[0]
    third = project_sum.shape[1]
    up_total, project_total, bias_sum, norms = jnp.split(
        everything[0], [units, units + third, units + third + width]
    )
    norms = sum_all(norms.reshape(4, width), (("tensor", 4),))
    return (
        layer_out,
        tokens_grad,
        project_grad.reshape(width // 4, 3, -1),
        project_total.reshape(3, -1),
        dense_grad,
        bias_sum,
        up_grad,
        up_total,
        down_grad,
        bias_sum,
        norms[0],
        norms[1],
        norms[2],
        norms[3],
    )


def solution(mesh):
    tokens = P(("fsdp", "context"), None)
    line = P(("fsdp", "context"))
    in_specs = (
        tokens, tokens, line, line, P("fsdp", None), tokens,
        P("fsdp", None, "tensor"), P(None, "tensor"), P("tensor", "fsdp"), P(),
        P("fsdp", "tensor"), P("tensor"), P("tensor", "fsdp"), P(), P(), P(), P(), P(),
    )
    out_specs = (
        tokens, tokens, P("fsdp", None, "tensor"), P(None, "tensor"), P("tensor", "fsdp"), P(),
        P("fsdp", "tensor"), P("tensor"), P("tensor", "fsdp"), P(), P(), P(), P(), P(),
    )
    run = partial(body, mesh.shape["context"])
    return jax.shard_map(run, mesh=mesh, in_specs=in_specs, out_specs=out_specs, check_vma=False)
```

time: 974 us -> 400 us (0.41)
  waiting for transfers between devices: 623 us -> 159 us
  matrix products: 142 us -> 13 us
  Pallas kernels: 0 us -> 76.6 us
  starting transfers between devices: 1.11 us -> 58.8 us
  loops' own time: 48.7 us -> 0 us
  blocking collectives: 32.7 us -> 0 us
  local copies, waits for them, and re-layouts: 52 us -> 30.6 us
    psum x2 -> x0, waiting for transfers between devices: 479 us -> none  [the longest x1 430 us: body(): summed = lax.psum(partial_out, 'tensor')]
    ppermute x0 -> x45, waiting for transfers between devices: none -> 158 us  [the longest x4 93.8 us: all_sum_rows(): got = lax.ppermute(final, 'tensor', [(1, 0), (2, 3)])]
    dot_general x66 -> x4, matrix products: 142 us -> 13 us  [body(): lax.dot_general(a, b, TN, preferred_element_type=f32).astype(bf16)]
    reduce_scatter x6 -> x1, waiting for transfers between devices: 110 us -> 0.02 us  [body(): lax.psum_scatter(partial_out, 'tensor', scatter_dimension=0, tiled=True)]
    pallas_call x0 -> x8, Pallas kernels: none -> 76.6 us  [the longest x2 22.2 us: attend_backward(): pl.pallas_call(partial(attend_backward_kernel, slots, maxk, split), grid=...]
    ppermute x0 -> x45, starting transfers between devices: none -> 58.8 us  [the longest x33 41.6 us: swap(): return jax.tree.map(lambda v: lax.ppermute(v, axis, pairs), values)]
    another operation x8 -> x0, loops' own time: 48.7 us -> none  [the longest x2 12.5 us: attend_forward(): (row_top, total), unused = lax.scan(first_pass, start_state, listing)]
    all_gather x5 -> x1, waiting for transfers between devices: 33.3 us -> 0.01 us  [body(): layer_out = lax.all_gather(layer_out, 'tensor', axis=0, tiled=True)]
  transfers between devices with their start and end apart: 13 -> 47, of which waited for: 8 -> 18; matrix products, arithmetic and copies ran while one was open for 23% -> 20% of each run, Pallas kernels for 0% -> 19%
where the time goes in v1:
time: 400 us; the launch traced here: 396 us
  waiting for transfers between devices  159 us (40%)
  Pallas kernels  76.6 us (19%)
  starting transfers between devices  58.8 us (15%)
  other arithmetic  43.5 us (11%)
  local copies, waits for them, and re-layouts  30.6 us (8%)
  between operations  15.1 us (4%)
  matrix products  13 us (3%)
    ppermute x4, waiting for transfers between devices, all_sum_rows(): got = lax.ppermute(final, 'tensor', [(1, 0), (2, 3)])  93.8 us
    ppermute x33, waiting for transfers between devices, swap(): return jax.tree.map(lambda v: lax.ppermute(v, axis, pairs), values)  42.4 us
    ppermute x33, starting transfers between devices, swap(): return jax.tree.map(lambda v: lax.ppermute(v, axis, pairs), values)  41.6 us
    ppermute x4, waiting for transfers between devices, all_sum_rows(): got = lax.ppermute(part, 'tensor', [(0, 1), (3, 2)])  22.3 us
    pallas_call x2, Pallas kernels, attend_backward(): pl.pallas_call(partial(attend_backward_kernel, slots, maxk, split), grid=...  22.2 us
    pallas_call x1, Pallas kernels, mlp_all(): pl.pallas_call(mlp_kernel, grid=(rows // tile,), in_specs=[smem, row(widt...  19 us
    pallas_call x2, Pallas kernels, attend_forward(): pl.pallas_call(partial(attend_forward_kernel, slots, maxk), grid=(), in_s...  14.6 us
    unnamed x82, local copies, waits for them, and re-layouts  13.8 us
  transfers between devices with their start and end apart: 47, of which 18 were waited for; matrix products, arithmetic and copies ran while one was open for 20% of the time, Pallas kernels for 19%

profile of v1, /device:TPU:0, one launch (start us, length us, event | category | flops | bytes accessed | tf_op | source)
XLA Modules:
  0.0 396.1 jit_solution(14168886204170989269)
XLA Ops:
  15.2 3.6 fusion
  18.8 3.4 fusion.17
  25.1 9.5 %collective-permute-done.9.d2 = bf16[1024,256]{1,0:T(8,128)(2,1)} collective-permute-done((bf16[1024,256]{1,0:T(8,128)(2,1)}, bf16[1024,256]{1,0:T(8,128)(2,1)}, u32[]{:S(2)}, u32[]{:S(2)}) %collective-permute-start.9) | collective-permute-done | bytes 524320 | tf_op jit(solution)/shard_map/ppermute | solution.py:435
  34.5 10.4 %collective-permute-done.6.u2 = bf16[256,1024]{1,0:T(8,128)(2,1)} collective-permute-done((bf16[256,1024]{1,0:T(8,128)(2,1)}, bf16[256,1024]{1,0:T(8,128)(2,1)}, u32[]{:S(2)}, u32[]{:S(2)}) %collective-permute-start.6) | collective-permute-done | bytes 524320 | tf_op jit(solution)/shard_map/ppermute | solution.py:435
  53.2 6.0 %project.1 = (bf16[1024,128]{1,0:T(8,128)(2,1)}, bf16[1024,128]{1,0:T(8,128)(2,1)}, bf16[1024,256]{1,0:T(8,128)(2,1)}, bf16[1024,256]{1,0:T(8,128)(2,1)}) custom-call(s32[4]{0:T(128)} %pad_add_fusion.ids, bf16[1024,1024]{1,0:T(8,128)(2,1)} %get-tuple-element.99.n1, bf16[3,256,256]{2,1,0:T(8,128)(2,1)} %bitcast.90, bf16[3,256,256]{2,1,0:T(8,128)(2,1)} %copy-done.16, ...), custom_call_target="tpu_custom_call" | custom-call | tf_op jit(solution)/shard_map/project/pallas_call | solution.py:80
  62.0 19.0 %mlp_all.1 = (bf16[1024,1024]{1,0:T(8,128)(2,1)}, bf16[1024,1024]{1,0:T(8,128)(2,1)}, bf16[1024,1024]{1,0:T(8,128)(2,1)}, f32[1024,1024]{1,0:T(8,128)}, f32[1024...) custom-call(s32[4]{0:T(128)} %pad_add_fusion.ids, ...), custom_call_target="tpu_custom_call" | custom-call | tf_op jit(solution)/shard_map/mlp_all/pallas_call | solution.py:324
  81.0 5.4 %convolution_convert_fusion = bf16[1024,1024]{0,1:T(8,128)(2,1)} fusion(bf16[1024,1024]{1,0:T(8,128)(2,1)} %get-tuple-element.71, bf16[1024,1024]{1,0:T(8,128)(2,1)S(1)} %copy-done.3), kind=kOutput, calls=%fused_computation.11 | convolution fusion | flops 2148532224 | bytes 6291456 | tf_op jit(solution)/shard_map/dot_general | solution.py:595
  86.4 3.9 copy.35
  93.5 7.5 %attend_forward.3 = (f32[1024,128]{1,0:T(8,128)}, f32[8,512]{1,0:T(8,128)}) custom-call(s32[8]{0:T(128)} %concatenate.9.ids, bf16[1024,128]{1,0:T(8,128)(2,1)} %get-tuple-element.46.q, bf16[1024,256]{1,0:T(8,128)(2,1)} %get-tuple-element.47.refs_0_, bf16[1024,256]{1,0:T(8,128)(2,1)} %copy-done.11), custom_call_target="tpu_custom_call" | custom-call | tf_op jit(solution)/shard_map/attend_forward/pallas_call | solution.py:160
  101.7 7.2 %attend_forward.2 = (f32[1024,128]{1,0:T(8,128)}, f32[8,512]{1,0:T(8,128)}) custom-call(s32[8]{0:T(128)} %concatenate.9.ids, bf16[1024,128]{1,0:T(8,128)(2,1)} %get-tuple-element.43.q, bf16[1024,256]{1,0:T(8,128)(2,1)} %get-tuple-element.44.refs_0_, bf16[1024,256]{1,0:T(8,128)(2,1)} %copy-done.10), custom_call_target="tpu_custom_call" | custom-call | tf_op jit(solution)/shard_map/attend_forward/pallas_call | solution.py:160
  108.9 5.3 %output_part.1 = (bf16[1024,1024]{1,0:T(8,128)(2,1)}, bf16[1024,256]{1,0:T(8,128)(2,1)}) custom-call(s32[4]{0:T(128)} %pad_add_fusion.ids, f32[1024,128]{1,0:T(8,128)} %get-tuple-element.45.o0.o, f32[1024,128]{1,0:T(8,128)} %get-tuple-element.48.o1.o, f32[1024,1024]{1,0:T(8,128)} %get-tuple-element.49.mlp, bf16[256,256]{1,0:T(8,128)(2,1)} %c0.3, ...), custom_call_target="tpu_custom_call" | custom-call | tf_op jit(solution)/shard_map/output_part/pallas_call | solution.py:355
  119.0 11.7 %attend_backward.3 = (f32[1024,256]{1,0:T(8,128)}, bf16[1024,256]{1,0:T(8,128)(2,1)}, bf16[1024,128]{1,0:T(8,128)(2,1)}) custom-call(s32[8]{0:T(128)} %concatenate.9.ids, bf16[1024,128]{1,0:T(8,128)(2,1)} %get-tuple-element.46.q, bf16[1024,128]{1,0:T(8,128)(2,1)} %get-tuple-element.55.g, f32[1024,128]{1,0:T(8,128)} %get-tuple-element.48.o1.o, ...), custom_call_target="tpu_custom_call" | custom-call | tf_op jit(solution)/shard_map/attend_backward/pallas_call | solution.py:261
  130.7 8.7 %collective-permute-start.15 = (bf16[1024,256]{1,0:T(8,128)(2,1)}, bf16[1024,256]{1,0:T(8,128)(2,1)S(1)}, u32[]{:S(2)}, u32[]{:S(2)}) collective-permute-start(bf16[1024,256]{1,0:T(8,128)(2,1)} %get-tuple-element.61), channel_id=1, source_target_pairs={{0,4},{4,0},{1,5},{5,1},{2,6},{6,2},{3,7},{7,3},{8,12},{12,8},{9,1... | collective-permute-start | bytes 1572872 | tf_op jit(solution)/shard_map/ppermute | solution.py:435
  139.3 10.5 %attend_backward.2 = (f32[1024,256]{1,0:T(8,128)}, bf16[1024,256]{1,0:T(8,128)(2,1)}, bf16[1024,128]{1,0:T(8,128)(2,1)}) custom-call(s32[8]{0:T(128)} %concatenate.9.ids, bf16[1024,128]{1,0:T(8,128)(2,1)} %get-tuple-element.43.q, bf16[1024,128]{1,0:T(8,128)(2,1)} %get-tuple-element.52.g, f32[1024,128]{1,0:T(8,128)} %get-tuple-element.45.o0.o, ...), custom_call_target="tpu_custom_call" | custom-call | tf_op jit(solution)/shard_map/attend_backward/pallas_call | solution.py:261
  152.6 3.1 collective-permute-start.37
  157.1 5.5 %collective-permute-done.14.refs_1_ = bf16[1024,256]{1,0:T(8,128)(2,1)S(1)} collective-permute-done((bf16[1024,256]{1,0:T(8,128)(2,1)}, bf16[1024,256]{1,0:T(8,128)(2,1)S(1)}, u32[]{:S(2)}, u32[]{:S(2)}) %collective-permute-start.14) | collective-permute-done | bytes 524320 | tf_op jit(solution)/shard_map/ppermute | solution.py:435
  163.4 9.4 %input_grad.1 = (bf16[1024,768]{1,0:T(8,128)(2,1)}, bf16[1024,1024]{1,0:T(8,128)(2,1)}, f32[8,1024]{1,0:T(8,128)}, f32[1,768]{1,0:T(1,128)}) custom-call(s32[4]{0:T(128)} %pad_add_fusion.ids, bf16[1024,1024]{1,0:T(8,128)(2,1)} %x.5, f32[1024,1024]{1,0:T(8,128)} %get-tuple-element.51.e2, f32[1,1024]{1,0:T(1,128)} %bitcast.94, ...), custom_call_target="tpu_custom_call" | custom-call | tf_op jit(solution)/shard_map/input_grad/pallas_call | solution.py:415
  176.6 3.9 collective-permute-start.31
  180.6 3.3 convolution_convert_fusion.2
  191.1 3.5 collective-permute-start.16
  201.2 6.8 %collective-permute-done.43 = f32[4,1024]{1,0:T(4,128)S(1)} collective-permute-done((f32[4,1024]{1,0:T(4,128)S(1)}, f32[4,1024]{1,0:T(4,128)S(1)}, u32[]{:S(2)}, u32[]{:S(2)}) %collective-permute-start.43) | collective-permute-done | bytes 16416 | tf_op jit(solution)/shard_map/ppermute | solution.py:435
  208.0 4.5 %collective-permute-start.44 = (f32[4,1024]{1,0:T(4,128)S(1)}, f32[4,1024]{1,0:T(4,128)S(1)}, u32[]{:S(2)}, u32[]{:S(2)}) collective-permute-start(f32[4,1024]{1,0:T(4,128)S(1)} %add.254), channel_id=1, source_target_pairs={{0,2},{1,3},{2,0},{3,1},{4,6},{5,7},{6,4},{7,5},{8,10},{9,11},{10,... | collective-permute-start | bytes 49160 | tf_op jit(solution)/shard_map/ppermute | solution.py:435
  225.8 3.9 collective-permute-done.19
  231.3 9.6 %collective-permute-done.22 = bf16[256,1024]{1,0:T(8,128)(2,1)S(1)} collective-permute-done((bf16[256,1024]{1,0:T(8,128)(2,1)}, bf16[256,1024]{1,0:T(8,128)(2,1)S(1)}, u32[]{:S(2)}, u32[]{:S(2)}) %collective-permute-start.22) | collective-permute-done | bytes 524320 | tf_op jit(solution)/shard_map/ppermute | solution.py:474
  240.9 8.8 %collective-permute-done.25 = bf16[256,1024]{1,0:T(8,128)(2,1)S(1)} collective-permute-done((bf16[256,1024]{1,0:T(8,128)(2,1)S(1)}, bf16[256,1024]{1,0:T(8,128)(2,1)S(1)}, u32[]{:S(2)}, u32[]{:S(2)}) %collective-permute-start.25) | collective-permute-done | bytes 524320 | tf_op jit(solution)/shard_map/ppermute | solution.py:474
  267.9 4.1 %fusion.8 = (bf16[256,1024]{1,0:T(8,128)(2,1)}, bf16[256,1024]{1,0:T(8,128)(2,1)}) fusion(f32[1024,1024]{1,0:T(8,128)} %convert_element_type.239, f32[1024,1024]{1,0:T(8,128)} %get-tuple-element.98, bf16[256,1024]{1,0:T(8,128)(2,1)} %copy-done.12, bf16[256,1024]{1,0:T(8,128)(2,1)S(1)} %get-tuple-element.100, f32[256]{0:T(256)S(1)} %broadcast_multiply_fusion.5, ...), kind=kLoop, calls=%fused_computation.22 | loop fusion | flops 4718592 | bytes 7346176 | tf_op jit(solution)/shard_map/convert_element_type | solution.py:591
  279.5 3.0 collective-permute-done.39
  288.8 30.3 %collective-permute-done.18 = bf16[256,1024]{1,0:T(8,128)(2,1)} collective-permute-done((bf16[256,1024]{1,0:T(8,128)(2,1)}, bf16[256,1024]{1,0:T(8,128)(2,1)}, u32[]{:S(2)}, u32[]{:S(2)}) %collective-permute-start.18) | collective-permute-done | bytes 524320 | tf_op jit(solution)/shard_map/ppermute | solution.py:478
  320.2 37.2 %collective-permute-done.21 = bf16[256,1024]{1,0:T(8,128)(2,1)S(1)} collective-permute-done((bf16[256,1024]{1,0:T(8,128)(2,1)}, bf16[256,1024]{1,0:T(8,128)(2,1)S(1)}, u32[]{:S(2)}, u32[]{:S(2)}) %collective-permute-start.21) | collective-permute-done | bytes 524320 | tf_op jit(solution)/shard_map/ppermute | solution.py:478
  357.4 17.7 %collective-permute-done.24 = bf16[256,1024]{1,0:T(8,128)(2,1)S(1)} collective-permute-done((bf16[256,1024]{1,0:T(8,128)(2,1)}, bf16[256,1024]{1,0:T(8,128)(2,1)S(1)}, u32[]{:S(2)}, u32[]{:S(2)}) %collective-permute-start.24) | collective-permute-done | bytes 524320 | tf_op jit(solution)/shard_map/ppermute | solution.py:478
  375.2 8.6 %collective-permute-done.27 = bf16[256,1024]{1,0:T(8,128)(2,1)S(1)} collective-permute-done((bf16[256,1024]{1,0:T(8,128)(2,1)S(1)}, bf16[256,1024]{1,0:T(8,128)(2,1)S(1)}, u32[]{:S(2)}, u32[]{:S(2)}) %collective-permute-start.27) | collective-permute-done | bytes 524320 | tf_op jit(solution)/shard_map/ppermute | solution.py:478
  386.0 3.1 copy.51
  (229 shorter events, 102.8 us)
Async XLA Ops:
  7.2 258.4 %reduce-scatter.2.cloned.1.call-start = ((), (), s32[]{:S(2)}) async-start(), calls=%async_computation.1 | async-start | bytes 2621440 | tf_op jit(solution)/shard_map/reduce_scatter | solution.py:562
  7.2 16.0 %collective-permute-start.1 = (bf16[3,256,256]{2,1,0:T(8,128)(2,1)}, bf16[3,256,256]{2,1,0:T(8,128)(2,1)S(1)}, u32[]{:S(2)}, u32[]{:S(2)}) collective-permute-start(bf16[3,256,256]{2,1,0:T(8,128)(2,1)} %bitcast.88), channel_id=1, source_target_pairs={{0,16},{8,24},{16,0},{24,8},{1,17},{9,25},{17,1},{25,9},{2,18},{10... | collective-permute-start | bytes 1179656 | tf_op jit(solution)/shard_map/ppermute | solution.py:435
  10.2 14.5 %collective-permute-start = (bf16[3,256,256]{2,1,0:T(8,128)(2,1)}, bf16[3,256,256]{2,1,0:T(8,128)(2,1)S(1)}, u32[]{:S(2)}, u32[]{:S(2)}) collective-permute-start(bf16[3,256,256]{2,1,0:T(8,128)(2,1)} %bitcast.89), channel_id=1, source_target_pairs={{0,8},{8,0},{16,24},{24,16},{1,9},{9,1},{17,25},{25,17},{2,10},{10... | collective-permute-start | bytes 1179656 | tf_op jit(solution)/shard_map/ppermute | solution.py:435
  10.4 24.1 %collective-permute-start.9 = (bf16[1024,256]{1,0:T(8,128)(2,1)}, bf16[1024,256]{1,0:T(8,128)(2,1)}, u32[]{:S(2)}, u32[]{:S(2)}) collective-permute-start(bf16[1024,256]{1,0:T(8,128)(2,1)} %d0.1), channel_id=1, source_target_pairs={{0,16},{8,24},{16,0},{24,8},{1,17},{9,25},{17,1},{25,9},{2,18},{10... | collective-permute-start | bytes 1572872 | tf_op jit(solution)/shard_map/ppermute | solution.py:435
  12.3 32.7 %collective-permute-start.6 = (bf16[256,1024]{1,0:T(8,128)(2,1)}, bf16[256,1024]{1,0:T(8,128)(2,1)}, u32[]{:S(2)}, u32[]{:S(2)}) collective-permute-start(bf16[256,1024]{1,0:T(8,128)(2,1)} %u0.1), channel_id=1, source_target_pairs={{0,16},{8,24},{16,0},{24,8},{1,17},{9,25},{17,1},{25,9},{2,18},{10... | collective-permute-start | bytes 1572872 | tf_op jit(solution)/shard_map/ppermute | solution.py:435
  23.2 23.0 %collective-permute-start.2 = (bf16[3,256,256]{2,1,0:T(8,128)(2,1)S(1)}, bf16[3,256,256]{2,1,0:T(8,128)(2,1)S(1)}, u32[]{:S(2)}, u32[]{:S(2)}) collective-permute-start(bf16[3,256,256]{2,1,0:T(8,128)(2,1)S(1)} %collective-permute-done.1.w2), channel_id=1, source_target_pairs={{0,8},{8,0},{16,24},{24,16},{1,9},{9,1},{17,25},{25,17},{2,10},{10... | collective-permute-start | bytes 1179656 | tf_op jit(solution)/shard_map/ppermute | solution.py:435
  24.6 37.1 %collective-permute-start.5 = (bf16[256,1024]{1,0:T(8,128)(2,1)}, bf16[256,1024]{1,0:T(8,128)(2,1)}, u32[]{:S(2)}, u32[]{:S(2)}) collective-permute-start(bf16[256,1024]{1,0:T(8,128)(2,1)} %u0.1), channel_id=1, source_target_pairs={{0,8},{8,0},{16,24},{24,16},{1,9},{9,1},{17,25},{25,17},{2,10},{10... | collective-permute-start | bytes 1572872 | tf_op jit(solution)/shard_map/ppermute | solution.py:435
  24.7 37.2 %collective-permute-start.8 = (bf16[1024,256]{1,0:T(8,128)(2,1)}, bf16[1024,256]{1,0:T(8,128)(2,1)}, u32[]{:S(2)}, u32[]{:S(2)}) collective-permute-start(bf16[1024,256]{1,0:T(8,128)(2,1)} %d0.1), channel_id=1, source_target_pairs={{0,8},{8,0},{16,24},{24,16},{1,9},{9,1},{17,25},{25,17},{2,10},{10... | collective-permute-start | bytes 1572872 | tf_op jit(solution)/shard_map/ppermute | solution.py:435
  34.5 27.4 %collective-permute-start.10 = (bf16[1024,256]{1,0:T(8,128)(2,1)}, bf16[1024,256]{1,0:T(8,128)(2,1)}, u32[]{:S(2)}, u32[]{:S(2)}) collective-permute-start(bf16[1024,256]{1,0:T(8,128)(2,1)} %collective-permute-done.9.d2), channel_id=1, source_target_pairs={{0,8},{8,0},{16,24},{24,16},{1,9},{9,1},{17,25},{25,17},{2,10},{10... | collective-permute-start | bytes 1572872 | tf_op jit(solution)/shard_map/ppermute | solution.py:435
  45.0 17.0 %collective-permute-start.7 = (bf16[256,1024]{1,0:T(8,128)(2,1)}, bf16[256,1024]{1,0:T(8,128)(2,1)}, u32[]{:S(2)}, u32[]{:S(2)}) collective-permute-start(bf16[256,1024]{1,0:T(8,128)(2,1)} %collective-permute-done.6.u2), channel_id=1, source_target_pairs={{0,8},{8,0},{16,24},{24,16},{1,9},{9,1},{17,25},{25,17},{2,10},{10... | collective-permute-start | bytes 1572872 | tf_op jit(solution)/shard_map/ppermute | solution.py:435
  59.9 32.7 %collective-permute-start.4 = (bf16[1024,256]{1,0:T(8,128)(2,1)}, bf16[1024,256]{1,0:T(8,128)(2,1)S(1)}, u32[]{:S(2)}, u32[]{:S(2)}) collective-permute-start(bf16[1024,256]{1,0:T(8,128)(2,1)} %get-tuple-element.47.refs_0_), channel_id=1, source_target_pairs={{0,4},{4,0},{1,5},{5,1},{2,6},{6,2},{3,7},{7,3},{8,12},{12,8},{9,1... | collective-permute-start | bytes 1572872 | tf_op jit(solution)/shard_map/ppermute | solution.py:435
  61.7 39.2 %collective-permute-start.3 = (bf16[1024,256]{1,0:T(8,128)(2,1)}, bf16[1024,256]{1,0:T(8,128)(2,1)S(1)}, u32[]{:S(2)}, u32[]{:S(2)}) collective-permute-start(bf16[1024,256]{1,0:T(8,128)(2,1)} %get-tuple-element.44.refs_0_), channel_id=1, source_target_pairs={{0,4},{4,0},{1,5},{5,1},{2,6},{6,2},{3,7},{7,3},{8,12},{12,8},{9,1... | collective-permute-start | bytes 1572872 | tf_op jit(solution)/shard_map/ppermute | solution.py:435
  92.6 125.0 %collective-permute-start.40 = (bf16[2,1024,256]{2,1,0:T(8,128)(2,1)}, bf16[2,1024,256]{2,1,0:T(8,128)(2,1)}, u32[]{:S(2)}, u32[]{:S(2)}) collective-permute-start(bf16[2,1024,256]{2,1,0:T(8,128)(2,1)} %dynamic-slice_bitcast_fusion), channel_id=1, source_target_pairs={{0,8},{8,0},{16,24},{24,16},{1,9},{9,1},{17,25},{25,17},{2,10},{10... | collective-permute-start | bytes 3145736 | tf_op jit(solution)/shard_map/ppermute | solution.py:435
  116.2 35.2 %collective-permute-start.34 = (bf16[2,256,256]{2,1,0:T(8,128)(2,1)S(1)}, bf16[2,256,256]{2,1,0:T(8,128)(2,1)S(1)}, u32[]{:S(2)}, u32[]{:S(2)}) collective-permute-start(bf16[2,256,256]{2,1,0:T(8,128)(2,1)S(1)} %dynamic-slice_bitcast_fusion.5), channel_id=1, source_target_pairs={{0,8},{8,0},{16,24},{24,16},{1,9},{9,1},{17,25},{25,17},{2,10},{10... | collective-permute-start | bytes 786440 | tf_op jit(solution)/shard_map/ppermute | solution.py:435
  130.7 26.4 %collective-permute-start.15 = (bf16[1024,256]{1,0:T(8,128)(2,1)}, bf16[1024,256]{1,0:T(8,128)(2,1)S(1)}, u32[]{:S(2)}, u32[]{:S(2)}) collective-permute-start(bf16[1024,256]{1,0:T(8,128)(2,1)} %get-tuple-element.61), channel_id=1, source_target_pairs={{0,4},{4,0},{1,5},{5,1},{2,6},{6,2},{3,7},{7,3},{8,12},{12,8},{9,1... | collective-permute-start | bytes 1572872 | tf_op jit(solution)/shard_map/ppermute | solution.py:435
  152.6 68.3 %collective-permute-start.37 = (bf16[2,256,1024]{2,1,0:T(8,128)(2,1)}, bf16[2,256,1024]{2,1,0:T(8,128)(2,1)}, u32[]{:S(2)}, u32[]{:S(2)}) collective-permute-start(bf16[2,256,1024]{2,1,0:T(8,128)(2,1)} %dynamic-slice_bitcast_fusion.1), channel_id=1, source_target_pairs={{0,8},{8,0},{16,24},{24,16},{1,9},{9,1},{17,25},{25,17},{2,10},{10... | collective-permute-start | bytes 3145736 | tf_op jit(solution)/shard_map/ppermute | solution.py:435
  155.7 229.7 %all-gather.2.cloned.1.call-start = ((), (), s32[]{:S(2)}) async-start(), calls=%async_computation.2 | async-start | bytes 2621440 | tf_op jit(solution)/shard_map/all_gather | solution.py:566
  156.5 38.7 %collective-permute-start.36 = (bf16[256,256]{1,0:T(8,128)(2,1)S(1)}, bf16[256,256]{1,0:T(8,128)(2,1)}, u32[]{:S(2)}, u32[]{:S(2)}) collective-permute-start(bf16[256,256]{1,0:T(8,128)(2,1)S(1)} %fusion.22), channel_id=1, source_target_pairs={{0,4},{4,0},{1,5},{5,1},{2,6},{6,2},{3,7},{7,3},{8,12},{12,8},{9,1... | collective-permute-start | bytes 393224 | tf_op jit(solution)/shard_map/ppermute | solution.py:435
  187.1 66.0 %collective-permute-start.28 = (bf16[2,256,768]{1,2,0:T(8,128)(2,1)}, bf16[2,256,768]{1,2,0:T(8,128)(2,1)}, u32[]{:S(2)}, u32[]{:S(2)}) collective-permute-start(bf16[2,256,768]{1,2,0:T(8,128)(2,1)} %bitcast.93), channel_id=1, source_target_pairs={{0,8},{8,0},{16,24},{24,16},{1,9},{9,1},{17,25},{25,17},{2,10},{10... | collective-permute-start | bytes 2359304 | tf_op jit(solution)/shard_map/ppermute | solution.py:435
  191.1 33.0 %collective-permute-start.16 = (bf16[256,1024]{1,0:T(8,128)(2,1)}, bf16[256,1024]{1,0:T(8,128)(2,1)S(1)}, u32[]{:S(2)}, u32[]{:S(2)}) collective-permute-start(bf16[256,1024]{1,0:T(8,128)(2,1)} %get-tuple-element.107), channel_id=1, source_target_pairs={{0,1},{3,2},{4,5},{7,6},{8,9},{11,10},{12,13},{15,14},{16,17},{19,... | collective-permute-start | bytes 1572872 | tf_op jit(solution)/shard_map/ppermute | solution.py:474
  214.2 15.4 %collective-permute-start.19 = (bf16[256,1024]{1,0:T(8,128)(2,1)}, bf16[256,1024]{1,0:T(8,128)(2,1)S(1)}, u32[]{:S(2)}, u32[]{:S(2)}) collective-permute-start(bf16[256,1024]{1,0:T(8,128)(2,1)} %get-tuple-element.104), channel_id=1, source_target_pairs={{0,1},{3,2},{4,5},{7,6},{8,9},{11,10},{12,13},{15,14},{16,17},{19,... | collective-permute-start | bytes 1572872 | tf_op jit(solution)/shard_map/ppermute | solution.py:474
  217.7 23.2 %collective-permute-start.22 = (bf16[256,1024]{1,0:T(8,128)(2,1)}, bf16[256,1024]{1,0:T(8,128)(2,1)S(1)}, u32[]{:S(2)}, u32[]{:S(2)}) collective-permute-start(bf16[256,1024]{1,0:T(8,128)(2,1)} %get-tuple-element.106), channel_id=1, source_target_pairs={{0,1},{3,2},{4,5},{7,6},{8,9},{11,10},{12,13},{15,14},{16,17},{19,... | collective-permute-start | bytes 1572872 | tf_op jit(solution)/shard_map/ppermute | solution.py:474
  221.0 28.7 %collective-permute-start.25 = (bf16[256,1024]{1,0:T(8,128)(2,1)S(1)}, bf16[256,1024]{1,0:T(8,128)(2,1)S(1)}, u32[]{:S(2)}, u32[]{:S(2)}) collective-permute-start(bf16[256,1024]{1,0:T(8,128)(2,1)S(1)} %copy-done.25), channel_id=1, source_target_pairs={{0,1},{3,2},{4,5},{7,6},{8,9},{11,10},{12,13},{15,14},{16,17},{19,... | collective-permute-start | bytes 1572872 | tf_op jit(solution)/shard_map/ppermute | solution.py:474
  224.1 31.2 %collective-permute-start.41 = (bf16[1024,256]{1,0:T(8,128)(2,1)S(1)}, bf16[1024,256]{1,0:T(8,128)(2,1)S(1)}, u32[]{:S(2)}, u32[]{:S(2)}) collective-permute-start(bf16[1024,256]{1,0:T(8,128)(2,1)S(1)} %dynamic-slice_bitcast_fusion.2), channel_id=1, source_target_pairs={{0,16},{8,24},{16,0},{24,8},{1,17},{9,25},{17,1},{25,9},{2,18},{10... | collective-permute-start | bytes 1572872 | tf_op jit(solution)/shard_map/ppermute | solution.py:435
  229.7 26.5 %collective-permute-start.38 = (bf16[256,1024]{1,0:T(8,128)(2,1)S(1)}, bf16[256,1024]{1,0:T(8,128)(2,1)S(1)}, u32[]{:S(2)}, u32[]{:S(2)}) collective-permute-start(bf16[256,1024]{1,0:T(8,128)(2,1)S(1)} %dynamic-slice_bitcast_fusion.3), channel_id=1, source_target_pairs={{0,16},{8,24},{16,0},{24,8},{1,17},{9,25},{17,1},{25,9},{2,18},{10... | collective-permute-start | bytes 1572872 | tf_op jit(solution)/shard_map/ppermute | solution.py:435
  256.2 19.6 %collective-permute-start.42 = (bf16[1024,256]{1,0:T(8,128)(2,1)S(1)}, bf16[1024,256]{1,0:T(8,128)(2,1)}, u32[]{:S(2)}, u32[]{:S(2)}) collective-permute-start(bf16[1024,256]{1,0:T(8,128)(2,1)S(1)} %fusion.10), channel_id=1, source_target_pairs={{0,4},{4,0},{1,5},{5,1},{2,6},{6,2},{3,7},{7,3},{8,12},{12,8},{9,1... | collective-permute-start | bytes 1572872 | tf_op jit(solution)/shard_map/ppermute | solution.py:435
  258.1 24.4 %collective-permute-start.39 = (bf16[256,1024]{1,0:T(8,128)(2,1)S(1)}, bf16[256,1024]{1,0:T(8,128)(2,1)}, u32[]{:S(2)}, u32[]{:S(2)}) collective-permute-start(bf16[256,1024]{1,0:T(8,128)(2,1)S(1)} %fusion.11), channel_id=1, source_target_pairs={{0,4},{4,0},{1,5},{5,1},{2,6},{6,2},{3,7},{7,3},{8,12},{12,8},{9,1... | collective-permute-start | bytes 1572872 | tf_op jit(solution)/shard_map/ppermute | solution.py:435
  258.6 14.8 %collective-permute-start.29 = (bf16[256,768]{0,1:T(8,128)(2,1)S(1)}, bf16[256,768]{0,1:T(8,128)(2,1)}, u32[]{:S(2)}, u32[]{:S(2)}) collective-permute-start(bf16[256,768]{0,1:T(8,128)(2,1)S(1)} %dynamic-slice_bitcast_fusion.4), channel_id=1, source_target_pairs={{0,16},{8,24},{16,0},{24,8},{1,17},{9,25},{17,1},{25,9},{2,18},{10... | collective-permute-start | bytes 1179656 | tf_op jit(solution)/shard_map/ppermute | solution.py:435
  264.3 54.8 %collective-permute-start.18 = (bf16[256,1024]{1,0:T(8,128)(2,1)}, bf16[256,1024]{1,0:T(8,128)(2,1)}, u32[]{:S(2)}, u32[]{:S(2)}) collective-permute-start(bf16[256,1024]{1,0:T(8,128)(2,1)} %get-tuple-element.94), channel_id=1, source_target_pairs={{1,0},{2,3},{5,4},{6,7},{9,8},{10,11},{13,12},{14,15},{17,16},{18,... | collective-permute-start | bytes 1572872 | tf_op jit(solution)/shard_map/ppermute | solution.py:478
  272.0 85.4 %collective-permute-start.21 = (bf16[256,1024]{1,0:T(8,128)(2,1)}, bf16[256,1024]{1,0:T(8,128)(2,1)S(1)}, u32[]{:S(2)}, u32[]{:S(2)}) collective-permute-start(bf16[256,1024]{1,0:T(8,128)(2,1)} %get-tuple-element.96), channel_id=1, source_target_pairs={{1,0},{2,3},{5,4},{6,7},{9,8},{10,11},{13,12},{14,15},{17,16},{18,... | collective-permute-start | bytes 1572872 | tf_op jit(solution)/shard_map/ppermute | solution.py:478
  273.4 101.8 %collective-permute-start.24 = (bf16[256,1024]{1,0:T(8,128)(2,1)}, bf16[256,1024]{1,0:T(8,128)(2,1)S(1)}, u32[]{:S(2)}, u32[]{:S(2)}) collective-permute-start(bf16[256,1024]{1,0:T(8,128)(2,1)} %get-tuple-element.97), channel_id=1, source_target_pairs={{1,0},{2,3},{5,4},{6,7},{9,8},{10,11},{13,12},{14,15},{17,16},{18,... | collective-permute-start | bytes 1572872 | tf_op jit(solution)/shard_map/ppermute | solution.py:478
  282.5 101.3 %collective-permute-start.27 = (bf16[256,1024]{1,0:T(8,128)(2,1)S(1)}, bf16[256,1024]{1,0:T(8,128)(2,1)S(1)}, u32[]{:S(2)}, u32[]{:S(2)}) collective-permute-start(bf16[256,1024]{1,0:T(8,128)(2,1)S(1)} %copy-done.14), channel_id=1, source_target_pairs={{1,0},{2,3},{5,4},{6,7},{9,8},{10,11},{13,12},{14,15},{17,16},{18,... | collective-permute-start | bytes 1572872 | tf_op jit(solution)/shard_map/ppermute | solution.py:478
  (51 other events, 656.9 us)
Sparse Core Ops, SparseCore 0:
  155.8 45.4 reduce-scatter.1
  268.0 102.7 all-gather.1
